TPU v7x, 32 devices: a whole 2x2x4 slice. The times are simulated.
32 devices in a mesh: blk: 4 (over y, core), grid: 8 (over z, x).
Axes of the slice: x: 2, y: 2, z: 4, core: 2. Of those that a mesh axis runs over, the one named last changes fastest.
Arguments:
- constraints: float32 [16384, 1024], P(('blk', 'grid')), may hold values from -0.1875 to 0.1875
- times_x: float32 [16384, 1024], P(('blk', 'grid')), may hold values from -6 to 6
- times_zinv: float32 [16384, 1024], P(('blk', 'grid')), may hold values from -6 to 6
- owner: int32 [4, 8, 8], P('blk', 'grid'), may hold values from 0 to 7, each once within a row
- update: float32 [4, 8, 8, 64, 1024], P('blk', 'grid'), may hold values from -6 to 6
Outputs:
- owned: float32 [4, 8, 8, 64, 1024], P('blk', 'grid')
Inputs may be any that keep to these rules, and one draw needn't show every extreme that they name: Each owner[b, g, :] is a permutation of 0 to 7.
All inputs are finite; a program needn't handle non-finite values.
Results may differ from a plain program's by a relative error of at most 0.0003.
Values sent between devices are 32-bit elements; how exact they have to be, the bound alone decides.
No kernel may reach another device: no remote copies, remote signals or barrier semaphores. Data moves between devices by JAX's collectives and lax.ppermute only.
A program may use at most 64 MiB of HBM per device.

v0:
```python
import jax
import jax.numpy as jnp
from jax import lax
from jax.sharding import PartitionSpec as P

ROUNDS = 2


def from_behind(array, axis, by):
    length = lax.axis_size(axis)
    return lax.ppermute(array, axis, [(i, (i + by) % length) for i in range(length)])


def hadamard_panel(rows_x, rows_z, panel):
    left = jnp.dot(
        rows_x, panel.T, preferred_element_type=jnp.float32, precision=lax.Precision.HIGHEST
    )
    right = jnp.dot(
        rows_z, panel.T, preferred_element_type=jnp.float32, precision=lax.Precision.HIGHEST
    )
    return left * right


def body(constraints, times_x, times_zinv, owner, update):
    groups = lax.axis_size("grid")
    row_count, width = times_x.shape
    tile_rows = row_count // groups
    places = jnp.arange(groups, dtype=jnp.int32)
    onehot = owner[0, 0][None, :] == places[:, None]
    inverse = jnp.sum(jnp.where(onehot, places[None, :], 0), axis=1)
    rows_x = times_x.reshape(groups, tile_rows, width)[inverse].reshape(row_count, width)
    rows_z = times_zinv.reshape(groups, tile_rows, width)[inverse].reshape(row_count, width)
    panel = constraints
    pieces = []
    for step in range(ROUNDS):
        if step > 0:
            panel = from_behind(panel, "blk", 1)
        block = hadamard_panel(rows_x, rows_z, panel).reshape(groups, tile_rows, panel.shape[0])
        pieces.append(lax.all_to_all(block, "grid", split_axis=0, concat_axis=0, tiled=True))
    joined = jnp.concatenate(pieces, axis=2)
    return joined[None, None] - update


def solution(mesh):
    placed = (
        P(("blk", "grid"), None),
        P(("blk", "grid"), None),
        P(("blk", "grid"), None),
        P("blk", "grid", None),
        P("blk", "grid", None, None, None),
    )
    return jax.shard_map(
        body,
        mesh=mesh,
        in_specs=placed,
        out_specs=P("blk", "grid", None, None, None),
        check_vma=False,
    )
```

profile of v0, /device:TPU:0, one launch (start us, length us, event | category | flops | bytes accessed | tf_op | source)
XLA Modules:
  0.0 83.1 jit_solution(3637008256526418632)
XLA Ops:
  0.0 0.0 copy-start
  0.0 0.5 collective-permute-start
  0.5 0.9 %select_reduce_fusion = s32[8]{0:T(128)S(1)} fusion(s32[8]{0:T(128)} %bitcast.31), kind=kLoop, calls=%fused_computation.7 | loop fusion | flops 184 | bytes 64 | tf_op jit(solution)/shard_map/reduce_sum | solution.py:30
  1.4 0.2 copy-done
  1.6 2.0 %gather_fusion.1 = f32[8,64,1024]{2,1,0:T(8,128)} fusion(f32[8,64,1024]{2,1,0:T(8,128)S(1)} %bitcast.23, s32[1024]{0:T(1024)S(1)} %pad_clamp_fusion), kind=kCustom, calls=%fused_computation.1 | custom fusion | bytes 4194336 | tf_op jit(solution)/shard_map/gather | solution.py:32
  3.6 3.6 %gather_fusion = f32[8,64,1024]{2,1,0:T(8,128)} fusion(f32[8,64,1024]{2,1,0:T(8,128)} %bitcast.30, s32[1024]{0:T(1024)S(1)} %pad_clamp_fusion), kind=kCustom, calls=%fused_computation | custom fusion | bytes 4194336 | tf_op jit(solution)/shard_map/gather | solution.py:31
  7.2 0.0 copy-start.2
  7.2 0.0 copy-start.3
  7.2 5.9 %fusion.2 = f32[512,512]{1,0:T(8,128)S(1)} fusion(f32[512,1024]{1,0:T(8,128)} %bitcast.24, f32[512,1024]{1,0:T(8,128)} %param.5), kind=kOutput, calls=%fused_computation.11 | convolution fusion | flops 3221225472 | bytes 5242880 | tf_op jit(solution)/shard_map/dot_general | solution.py:15
  13.1 0.0 copy-done.2
  13.1 0.0 copy-done.3
  13.1 4.6 %convolution_multiply_fusion.1 = f32[512,512]{1,0:T(8,128)} fusion(f32[512,512]{1,0:T(8,128)S(1)} %fusion.2, f32[512,1024]{1,0:T(8,128)S(1)} %bitcast.27, f32[512,1024]{1,0:T(8,128)S(1)} %copy-done.3), kind=kOutput, calls=%fused_computation.5 | convolution fusion | flops 3221487616 | bytes 6291456 | tf_op jit(solution)/shard_map/dot_general | solution.py:18
  17.6 7.3 %all-to-all-start = ((f32[8,64,512]{2,1,0:T(8,128)}), f32[8,64,512]{2,1,0:T(8,128)S(1)}, u32[]{:S(2)}, u32[]{:S(2)}) async-start(f32[8,64,512]{2,1,0:T(8,128)} %bitcast.28), calls=%async_computation | async-start | bytes 2097152 | tf_op jit(solution)/shard_map/all_to_all | solution.py:39
  24.9 0.0 copy-start.1
  24.9 1.5 %collective-permute-done = f32[512,1024]{1,0:T(8,128)} collective-permute-done((f32[512,1024]{1,0:T(8,128)}, f32[512,1024]{1,0:T(8,128)}, u32[]{:S(2)}, u32[]{:S(2)}) %collective-permute-start) | collective-permute-done | bytes 2097184 | tf_op jit(solution)/shard_map/ppermute | solution.py:11
  26.4 5.7 %fusion.3 = f32[512,512]{1,0:T(8,128)S(1)} fusion(f32[512,1024]{1,0:T(8,128)} %bitcast.26, f32[512,1024]{1,0:T(8,128)} %collective-permute-done), kind=kOutput, calls=%fused_computation.12 | convolution fusion | flops 3221225472 | bytes 5242880 | tf_op jit(solution)/shard_map/dot_general | solution.py:18
  32.2 0.0 copy-done.1
  32.2 6.1 %convolution_multiply_fusion = f32[512,512]{1,0:T(8,128)} fusion(f32[512,512]{1,0:T(8,128)S(1)} %fusion.3, f32[512,1024]{1,0:T(8,128)S(1)} %bitcast.25, f32[512,1024]{1,0:T(8,128)} %collective-permute-done), kind=kOutput, calls=%fused_computation.4 | convolution fusion | flops 3221487616 | bytes 6291456 | tf_op jit(solution)/shard_map/dot_general | solution.py:15
  38.3 13.3 %all-to-all-done = f32[8,64,512]{2,1,0:T(8,128)S(1)} async-done(((f32[8,64,512]{2,1,0:T(8,128)}), f32[8,64,512]{2,1,0:T(8,128)S(1)}, u32[]{:S(2)}, u32[]{:S(2)}) %all-to-all-start) | async-done | bytes 1048608 | tf_op jit(solution)/shard_map/all_to_all | solution.py:39
  51.7 0.0 copy-start.4
  51.7 29.7 %all_to_all.10 = f32[8,64,512]{2,1,0:T(8,128)S(1)} all-to-all(f32[8,64,512]{2,1,0:T(8,128)} %bitcast.29), channel_id=1, replica_groups=mesh['blk'=4,'grid'=8] {'grid'}, dimensions={0} | all-to-all | bytes 2097152 | tf_op jit(solution)/shard_map/all_to_all | solution.py:39
  81.4 0.0 copy-done.4
  81.4 1.7 %fusion = f32[1,1,8,64,1024]{4,3,2,1,0:T(8,128)} fusion(f32[1,1,8,64,1024]{4,3,2,1,0:T(8,128)S(1)} %copy-done.4, f32[8,64,512]{2,1,0:T(8,128)S(1)} %all_to_all.10, f32[8,64,512]{2,1,0:T(8,128)S(1)} %all-to-all-done), kind=kLoop, calls=%fused_computation.3 | loop fusion | flops 1048576 | bytes 6291456 | tf_op jit(solution)/shard_map/sub | solution.py:41
  (2 shorter events, 0.0 us)
Async XLA Ops:
  0.0 1.6 %copy-start = (f32[512,1024]{1,0:T(8,128)S(1)}, f32[512,1024]{1,0:T(8,128)}, u32[]{:S(2)}) copy-start(f32[512,1024]{1,0:T(8,128)} %param.7) | copy-start | bytes 6291460
  0.0 26.4 %collective-permute-start = (f32[512,1024]{1,0:T(8,128)}, f32[512,1024]{1,0:T(8,128)}, u32[]{:S(2)}, u32[]{:S(2)}) collective-permute-start(f32[512,1024]{1,0:T(8,128)} %param.5), channel_id=1, source_target_pairs={{0,8},{8,16},{16,24},{24,0},{1,9},{9,17},{17,25},{25,1},{2,10},{10... | collective-permute-start | bytes 6291464 | tf_op jit(solution)/shard_map/ppermute | solution.py:11
  7.2 5.9 %copy-start.2 = (f32[8,64,1024]{2,1,0:T(8,128)S(1)}, f32[8,64,1024]{2,1,0:T(8,128)}, u32[]{:S(2)}) copy-start(f32[8,64,1024]{2,1,0:T(8,128)} %gather_fusion.1) | copy-start | bytes 6291460
  7.2 5.9 %copy-start.3 = (f32[512,1024]{1,0:T(8,128)S(1)}, f32[512,1024]{1,0:T(8,128)}, u32[]{:S(2)}) copy-start(f32[512,1024]{1,0:T(8,128)} %param.5) | copy-start | bytes 6291460
  17.6 34.0 %all-to-all-start = ((f32[8,64,512]{2,1,0:T(8,128)}), f32[8,64,512]{2,1,0:T(8,128)S(1)}, u32[]{:S(2)}, u32[]{:S(2)}) async-start(f32[8,64,512]{2,1,0:T(8,128)} %bitcast.28), calls=%async_computation | async-start | bytes 2097152 | tf_op jit(solution)/shard_map/all_to_all | solution.py:39
  24.9 7.3 %copy-start.1 = (f32[8,64,1024]{2,1,0:T(8,128)S(1)}, f32[8,64,1024]{2,1,0:T(8,128)}, u32[]{:S(2)}) copy-start(f32[8,64,1024]{2,1,0:T(8,128)} %gather_fusion) | copy-start | bytes 6291460
  51.7 29.7 %copy-start.4 = (f32[1,1,8,64,1024]{4,3,2,1,0:T(8,128)S(1)}, f32[1,1,8,64,1024]{4,3,2,1,0:T(8,128)}, u32[]{:S(2)}) copy-start(f32[1,1,8,64,1024]{4,3,2,1,0:T(8,128)} %param.9) | copy-start | bytes 6291460
where the time goes:
time: 83.4 us; the launch traced here: 83.1 us
  blocking collectives  29.7 us (36%)
  matrix products  22.3 us (27%)
  waiting for transfers between devices  14.9 us (18%)
  starting transfers between devices  7.71 us (9%)
  local copies, waits for them, and re-layouts  5.76 us (7%)
  other arithmetic  2.68 us (3%)
    all_to_all x1, blocking collectives, body(): lax.all_to_all(block, 'grid', split_axis=0, concat_axis=0, tiled=True)  29.7 us
    all_to_all x1, waiting for transfers between devices, body(): lax.all_to_all(block, 'grid', split_axis=0, concat_axis=0, tiled=True)  13.3 us
    dot_general x2, matrix products, hadamard_panel(): jnp.dot(rows_x, panel.T, preferred_element_type=jnp.float32, precision=la...  12 us
    dot_general x2, matrix products, hadamard_panel(): jnp.dot(rows_z, panel.T, preferred_element_type=jnp.float32, precision=la...  10.3 us
    all_to_all x1, starting transfers between devices, body(): lax.all_to_all(block, 'grid', split_axis=0, concat_axis=0, tiled=True)  7.26 us
    gather x1, local copies, waits for them, and re-layouts, body(): times_x.reshape(groups, tile_rows, width)[inverse].reshape(row_count, width)  3.57 us
    gather x1, local copies, waits for them, and re-layouts, body(): times_zinv.reshape(groups, tile_rows, width)[inverse]  2 us
    sub x1, other arithmetic, body(): return joined[None, None] - update  1.72 us
  transfers between devices with their start and end apart: 2, of which 2 were waited for; matrix products, arithmetic and copies ran while one was open for 35% of the time, Pallas kernels for 0%

commit v1 on v0

v1 whole, which is shorter than its diff:
```python
import functools

import jax
import jax.numpy as jnp
from jax import lax
from jax.experimental import pallas as pl
from jax.experimental.pallas import tpu as pltpu
from jax.sharding import PartitionSpec as P

ROUNDS = 2
HALVES = 2
NT = (((1,), (1,)), ((), ()))
ANY = pl.BlockSpec(memory_space=pl.ANY)
SMEM = pl.BlockSpec(memory_space=pltpu.SMEM)
VMEM = pl.BlockSpec(memory_space=pltpu.VMEM)


def partner(me, j, groups):
    if groups & (groups - 1) == 0:
        return me ^ j
    return lax.rem(me + j, groups)


def exchange(piece, j, groups):
    if j == 0:
        return piece
    if groups & (groups - 1) == 0:
        pairs = [(i, i ^ j) for i in range(groups)]
    else:
        pairs = [(i, (i + j) % groups) for i in range(groups)]
    return lax.ppermute(piece, "grid", pairs)


def source(me, j, groups):
    if groups & (groups - 1) == 0:
        return me ^ j
    return lax.rem(me + groups - j, groups)


def split(x):
    high = x.astype(jnp.bfloat16)
    return high, (x - high.astype(jnp.float32)).astype(jnp.bfloat16)


def tiles_kernel(js, groups, owner, x_hbm, z_hbm, panel_hbm, *refs):
    outs, (rows, panel, row_sem, panel_sem) = refs[: len(js)], refs[len(js) :]
    tile = outs[0].shape[0]
    me = lax.axis_index("grid")
    copies = []
    fetch = pltpu.make_async_copy(panel_hbm, panel, panel_sem)
    fetch.start()
    for i, j in enumerate(js):
        to = partner(me, j, groups)
        t = jnp.int32(0)
        for k in range(groups):
            t = t + jnp.where(owner[0, 0, k] == to, k, 0)
        at = pl.ds(pl.multiple_of(t * tile, tile), tile)
        for s, hbm in enumerate((x_hbm, z_hbm)):
            place = pl.ds((s * len(js) + i) * tile, tile)
            copy = pltpu.make_async_copy(hbm.at[at], rows.at[place], row_sem.at[s, i])
            copy.start()
            copies.append(copy)
    for copy in copies:
        copy.wait()
    a_hi, a_lo = split(rows[...])
    fetch.wait()
    c_hi, c_lo = split(panel[...])
    dot = functools.partial(lax.dot_general, dimension_numbers=NT, preferred_element_type=jnp.float32)
    both = dot(a_hi, c_hi) + (dot(a_lo, c_hi) + dot(a_hi, c_lo))
    for i, out in enumerate(outs):
        left = both[i * tile : (i + 1) * tile]
        right = both[(len(js) + i) * tile : (len(js) + i + 1) * tile]
        out[...] = left * right


def tiles(js, groups, owner, times_x, times_zinv, panel):
    rows, width = times_x.shape
    tile = rows // groups
    cols = panel.shape[0]
    n = len(js)
    return pl.pallas_call(
        functools.partial(tiles_kernel, js, groups),
        out_shape=[jax.ShapeDtypeStruct((tile, cols), jnp.float32)] * n,
        in_specs=[SMEM, ANY, ANY, ANY],
        out_specs=[VMEM] * n,
        scratch_shapes=[
            pltpu.VMEM((2 * n * tile, width), jnp.float32),
            pltpu.VMEM((cols, width), jnp.float32),
            pltpu.SemaphoreType.DMA((2, n)),
            pltpu.SemaphoreType.DMA,
        ],
        compiler_params=pltpu.CompilerParams(vmem_limit_bytes=32 << 20),
        cost_estimate=pl.CostEstimate(
            flops=12 * n * tile * cols * width,
            bytes_accessed=4 * (2 * n * tile * width + cols * width + n * tile * cols),
            transcendentals=0,
        ),
        name="tiles_" + "_".join(map(str, js)),
    )(owner, times_x, times_zinv, panel)


def combine_kernel(js, groups, start, size, first, *refs):
    pieces = refs[: len(js)]
    update = refs[len(js)]
    out, u_buf, o_buf, u_sem, o_sem = refs[len(js) + (1 if first else 2) :]
    me = lax.axis_index("grid")
    loads, stores = [], []
    for i, j in enumerate(js):
        at = source(me, j, groups)
        copy = pltpu.make_async_copy(update.at[at, :, pl.ds(start, size)], u_buf.at[i], u_sem.at[i])
        copy.start()
        loads.append(copy)
    for i, j in enumerate(js):
        loads[i].wait()
        o_buf[i] = pieces[i][...] - u_buf[i]
        at = source(me, j, groups)
        copy = pltpu.make_async_copy(o_buf.at[i], out.at[at, :, pl.ds(start, size)], o_sem.at[i])
        copy.start()
        stores.append(copy)
    for copy in stores:
        copy.wait()


def combine(js, groups, start, pieces, update, out):
    tile, size = pieces[0].shape
    n = len(js)
    operands = list(pieces) + [update] + ([] if out is None else [out])
    return pl.pallas_call(
        functools.partial(combine_kernel, js, groups, start, size, out is None),
        out_shape=jax.ShapeDtypeStruct(update.shape, update.dtype),
        in_specs=[VMEM] * n + [ANY] * (len(operands) - n),
        out_specs=ANY,
        scratch_shapes=[
            pltpu.VMEM((n, tile, size), jnp.float32),
            pltpu.VMEM((n, tile, size), jnp.float32),
            pltpu.SemaphoreType.DMA((n,)),
            pltpu.SemaphoreType.DMA((n,)),
        ],
        input_output_aliases={} if out is None else {n + 1: 0},
        compiler_params=pltpu.CompilerParams(vmem_limit_bytes=16 << 20),
        cost_estimate=pl.CostEstimate(
            flops=n * tile * size, bytes_accessed=12 * n * tile * size, transcendentals=0
        ),
        name="combine",
    )(*operands)


def from_behind(array, axis, by):
    length = lax.axis_size(axis)
    return lax.ppermute(array, axis, [(i, (i + by) % length) for i in range(length)])


def body(constraints, times_x, times_zinv, owner, update):
    groups = lax.axis_size("grid")
    rows, width = times_x.shape
    update = update[0, 0]
    far = [j for j in range(groups // 2, groups)]
    near = [j for j in range(groups // 2 - 1, -1, -1)]
    pick = functools.partial(tiles, groups=groups, owner=owner, times_x=times_x, times_zinv=times_zinv)
    panel = constraints
    out = None
    start = 0
    for step in range(ROUNDS):
        if step > 0:
            panel = from_behind(panel, "blk", 1)
        sets = (far[:1], far[1:], near) if step == 0 else (far, near)
        js, pieces = [], []
        for some in sets:
            for j, piece in zip(some, pick(some, panel=panel)):
                js.append(j)
                pieces.append(exchange(piece, j, groups))
        out = combine(js, groups, start, pieces, update, out)
        start += panel.shape[0]
    return out[None, None]


def solution(mesh):
    placed = (
        P(("blk", "grid"), None),
        P(("blk", "grid"), None),
        P(("blk", "grid"), None),
        P("blk", "grid", None),
        P("blk", "grid", None, None, None),
    )
    return jax.shard_map(
        body,
        mesh=mesh,
        in_specs=placed,
        out_specs=P("blk", "grid", None, None, None),
        check_vma=False,
    )
```

time: 83.4 us -> 61.7 us (0.74)
  blocking collectives: 29.7 us -> 0 us
  matrix products: 22.3 us -> 0 us
  starting transfers between devices: 7.71 us -> 26.4 us
  Pallas kernels: 0 us -> 16.9 us
  other arithmetic: 2.68 us -> 0 us
  waiting for transfers between devices: 14.9 us -> 12.7 us
    all_to_all x1 -> x0, blocking collectives: 29.7 us -> none  [body(): lax.all_to_all(block, 'grid', split_axis=0, concat_axis=0, tiled=True)]
    ppermute x0 -> x14, starting transfers between devices: none -> 26 us  [exchange(): return lax.ppermute(piece, 'grid', pairs)]
    dot_general x4 -> x0, matrix products: 22.3 us -> none  [the longest x2 12 us: hadamard_panel(): jnp.dot(rows_x, panel.T, preferred_element_type=jnp.float32, precision=la...]
    pallas_call x0 -> x7, Pallas kernels: none -> 16.9 us  [the longest x5 14.3 us: tiles(): pl.pallas_call(functools.partial(tiles_kernel, js, groups), out_shape=[ja...]
    all_to_all x1 -> x0, waiting for transfers between devices: 13.3 us -> none  [body(): lax.all_to_all(block, 'grid', split_axis=0, concat_axis=0, tiled=True)]
    ppermute x0 -> x14, waiting for transfers between devices: none -> 8.69 us  [exchange(): return lax.ppermute(piece, 'grid', pairs)]
    all_to_all x1 -> x0, starting transfers between devices: 7.26 us -> none  [body(): lax.all_to_all(block, 'grid', split_axis=0, concat_axis=0, tiled=True)]
    gather x2 -> x0, local copies, waits for them, and re-layouts: 5.57 us -> none  [the longest x1 3.57 us: body(): times_x.reshape(groups, tile_rows, width)[inverse].reshape(row_count, width)]
  transfers between devices with their start and end apart: 2 -> 15, of which waited for: 2 -> 5; matrix products, arithmetic and copies ran while one was open for 35% -> 0% of each run, Pallas kernels for 0% -> 25%
where the time goes in v1:
time: 61.7 us; the launch traced here: 61.5 us
  starting transfers between devices  26.4 us (43%)
  Pallas kernels  16.9 us (27%)
  waiting for transfers between devices  12.7 us (21%)
  local copies, waits for them, and re-layouts  5.43 us (9%)
    ppermute x14, starting transfers between devices, exchange(): return lax.ppermute(piece, 'grid', pairs)  26 us
    pallas_call x5, Pallas kernels, tiles(): pl.pallas_call(functools.partial(tiles_kernel, js, groups), out_shape=[ja...  14.3 us
    ppermute x14, waiting for transfers between devices, exchange(): return lax.ppermute(piece, 'grid', pairs)  8.69 us
    unnamed x10, local copies, waits for them, and re-layouts  5.43 us
    ppermute x1, waiting for transfers between devices, from_behind(): lax.ppermute(array, axis, [(i, (i + by) % length) for i in range(length)])  3.97 us
    pallas_call x2, Pallas kernels, combine(): pl.pallas_call(functools.partial(combine_kernel, js, groups, start, size,...  2.58 us
  transfers between devices with their start and end apart: 15, of which 5 were waited for; matrix products, arithmetic and copies ran while one was open for 0% of the time, Pallas kernels for 25%

profile of v1, /device:TPU:0, one launch (start us, length us, event | category | flops | bytes accessed | tf_op | source)
XLA Modules:
  0.0 61.5 jit_solution(11151024420622984584)
XLA Ops:
  0.0 0.5 collective-permute-start
  0.5 0.0 copy-start
  0.5 1.6 %copy-done = f32[512,1024]{1,0:T(8,128)S(1)} copy-done((f32[512,1024]{1,0:T(8,128)S(1)}, f32[512,1024]{1,0:T(8,128)}, u32[]{:S(2)}) %copy-start) | copy-done | bytes 2097176
  2.0 0.0 copy-start.1
  2.0 1.6 %copy-done.1 = f32[512,1024]{1,0:T(8,128)S(1)} copy-done((f32[512,1024]{1,0:T(8,128)S(1)}, f32[512,1024]{1,0:T(8,128)}, u32[]{:S(2)}) %copy-start.1) | copy-done | bytes 2097176
  3.6 0.0 copy-start.2
  3.6 1.6 %copy-done.2 = f32[512,1024]{1,0:T(8,128)S(1)} copy-done((f32[512,1024]{1,0:T(8,128)S(1)}, f32[512,1024]{1,0:T(8,128)}, u32[]{:S(2)}) %copy-start.2) | copy-done | bytes 2097176
  5.2 0.0 copy-start.4
  5.2 0.7 %copy-done.4 = s32[1,1,8]{2,1,0:T(1,128)S(1)} copy-done((s32[1,1,8]{2,1,0:T(1,128)S(1)}, s32[1,1,8]{2,1,0:T(1,128)}, u32[]{:S(2)}) %copy-start.4) | copy-done | bytes 56
  5.9 2.0 %tiles_4.1 = f32[64,512]{1,0:T(8,128)S(1)} custom-call(s32[1,1,8]{2,1,0:T(1,128)S(1)} %copy-done.4, f32[512,1024]{1,0:T(8,128)S(1)} %copy-done, f32[512,1024]{1,0:T(8,128)S(1)} %copy-done.1, f32[512,1024]{1,0:T(8,128)S(1)} %copy-done.2), custom_call_target="tpu_custom_call" | custom-call | flops 402653184 | bytes 2752512 | tf_op jit(solution)/shard_map/tiles_4/pallas_call | solution.py:81
  7.9 3.7 %collective-permute-start.8 = (f32[64,512]{1,0:T(8,128)S(1)}, f32[64,512]{1,0:T(8,128)S(1)}, u32[]{:S(2)}, u32[]{:S(2)}) collective-permute-start(f32[64,512]{1,0:T(8,128)S(1)} %tiles_4.1), channel_id=1, source_target_pairs={{0,4},{1,5},{2,6},{3,7},{4,0},{5,1},{6,2},{7,3},{8,12},{9,13},{10,... | collective-permute-start | bytes 393224 | tf_op jit(solution)/shard_map/ppermute | solution.py:31
  11.6 2.6 %tiles_5_6_7.1 = (f32[64,512]{1,0:T(8,128)S(1)}, f32[64,512]{1,0:T(8,128)S(1)}, f32[64,512]{1,0:T(8,128)S(1)}) custom-call(s32[1,1,8]{2,1,0:T(1,128)S(1)} %copy-done.4, f32[512,1024]{1,0:T(8,128)S(1)} %copy-done, f32[512,1024]{1,0:T(8,128)S(1)} %copy-done.1, f32[512,1024]{1,0:T(8,128)S(1)} %copy-done.2), custom_call_target="tpu_custom_call" | custom-call | flops 1207959552 | bytes 4063232 | tf_op jit(solution)/shard_map/tiles_5_6_7/pallas_call | solution.py:81
  14.2 1.3 %collective-permute-start.9 = (f32[64,512]{1,0:T(8,128)S(1)}, f32[64,512]{1,0:T(8,128)S(1)}, u32[]{:S(2)}, u32[]{:S(2)}) collective-permute-start(f32[64,512]{1,0:T(8,128)S(1)} %get-tuple-element.28), channel_id=1, source_target_pairs={{0,5},{1,4},{2,7},{3,6},{4,1},{5,0},{6,3},{7,2},{8,13},{9,12},{10,... | collective-permute-start | bytes 393224 | tf_op jit(solution)/shard_map/ppermute | solution.py:31
  15.5 3.6 %collective-permute-start.10 = (f32[64,512]{1,0:T(8,128)S(1)}, f32[64,512]{1,0:T(8,128)S(1)}, u32[]{:S(2)}, u32[]{:S(2)}) collective-permute-start(f32[64,512]{1,0:T(8,128)S(1)} %get-tuple-element.29), channel_id=1, source_target_pairs={{0,6},{1,7},{2,4},{3,5},{4,2},{5,3},{6,0},{7,1},{8,14},{9,15},{10,... | collective-permute-start | bytes 393224 | tf_op jit(solution)/shard_map/ppermute | solution.py:31
  19.1 0.0 collective-permute-start.11
  19.1 3.2 %tiles_3_2_1_0.3 = (f32[64,512]{1,0:T(8,128)S(1)}, f32[64,512]{1,0:T(8,128)S(1)}, f32[64,512]{1,0:T(8,128)S(1)}, f32[64,512]{1,0:T(8,128)S(1)}) custom-call(s32[1,1,8]{2,1,0:T(1,128)S(1)} %copy-done.4, f32[512,1024]{1,0:T(8,128)S(1)} %copy-done, f32[512,1024]{1,0:T(8,128)S(1)} %copy-done.1, f32[512,1024]{1,0:T(8,128)S(1)} %copy-done.2), custom_call_target="tpu_custom_call" | custom-call | flops 1610612736 | bytes 4718592 | tf_op jit(solution)/shard_map/tiles_3_2_1_0/pallas_call | solution.py:81
  22.4 4.0 %collective-permute-done.panel_hbm = f32[512,1024]{1,0:T(8,128)S(1)} collective-permute-done((f32[512,1024]{1,0:T(8,128)}, f32[512,1024]{1,0:T(8,128)S(1)}, u32[]{:S(2)}, u32[]{:S(2)}) %collective-permute-start) | collective-permute-done | bytes 2097184 | tf_op jit(solution)/shard_map/ppermute | solution.py:150
  26.3 3.3 %collective-permute-start.12 = (f32[64,512]{1,0:T(8,128)S(1)}, f32[64,512]{1,0:T(8,128)S(1)}, u32[]{:S(2)}, u32[]{:S(2)}) collective-permute-start(f32[64,512]{1,0:T(8,128)S(1)} %get-tuple-element.31), channel_id=1, source_target_pairs={{0,3},{1,2},{2,1},{3,0},{4,7},{5,6},{6,5},{7,4},{8,11},{9,10},{10,... | collective-permute-start | bytes 393224 | tf_op jit(solution)/shard_map/ppermute | solution.py:31
  29.6 3.2 %tiles_4_5_6_7.1 = (f32[64,512]{1,0:T(8,128)S(1)}, f32[64,512]{1,0:T(8,128)S(1)}, f32[64,512]{1,0:T(8,128)S(1)}, f32[64,512]{1,0:T(8,128)S(1)}) custom-call(s32[1,1,8]{2,1,0:T(1,128)S(1)} %copy-done.4, f32[512,1024]{1,0:T(8,128)S(1)} %copy-done, f32[512,1024]{1,0:T(8,128)S(1)} %copy-done.1, f32[512,1024]{1,0:T(8,128)S(1)} %collective-permute-done.panel_hbm), custom_call_target="tpu_custom_call" | custom-call | flops 1610612736 | bytes 4718592 | tf_op jit(solution)/shard_map/tiles_4_5_6_7/pallas_call | solution.py:81
  32.9 0.0 collective-permute-done.8.refs_0_
  32.9 0.5 collective-permute-start.13
  33.4 0.0 collective-permute-done.9.refs_1_
  33.4 0.2 collective-permute-start.14
  33.6 0.0 collective-permute-done.10.refs_2_
  33.6 2.9 %collective-permute-start.1 = (f32[64,512]{1,0:T(8,128)S(1)}, f32[64,512]{1,0:T(8,128)S(1)}, u32[]{:S(2)}, u32[]{:S(2)}) collective-permute-start(f32[64,512]{1,0:T(8,128)S(1)} %get-tuple-element.20), channel_id=1, source_target_pairs={{0,4},{1,5},{2,6},{3,7},{4,0},{5,1},{6,2},{7,3},{8,12},{9,13},{10,... | collective-permute-start | bytes 393224 | tf_op jit(solution)/shard_map/ppermute | solution.py:31
  36.5 0.0 collective-permute-done.11.refs_3_
  36.5 0.0 copy-start.3
  36.5 2.9 %collective-permute-start.2 = (f32[64,512]{1,0:T(8,128)S(1)}, f32[64,512]{1,0:T(8,128)S(1)}, u32[]{:S(2)}, u32[]{:S(2)}) collective-permute-start(f32[64,512]{1,0:T(8,128)S(1)} %get-tuple-element.21), channel_id=1, source_target_pairs={{0,5},{1,4},{2,7},{3,6},{4,1},{5,0},{6,3},{7,2},{8,13},{9,12},{10,... | collective-permute-start | bytes 393224 | tf_op jit(solution)/shard_map/ppermute | solution.py:31
  39.4 3.2 %tiles_3_2_1_0.2 = (f32[64,512]{1,0:T(8,128)S(1)}, f32[64,512]{1,0:T(8,128)S(1)}, f32[64,512]{1,0:T(8,128)S(1)}, f32[64,512]{1,0:T(8,128)S(1)}) custom-call(s32[1,1,8]{2,1,0:T(1,128)S(1)} %copy-done.4, f32[512,1024]{1,0:T(8,128)S(1)} %copy-done, f32[512,1024]{1,0:T(8,128)S(1)} %copy-done.1, f32[512,1024]{1,0:T(8,128)S(1)} %collective-permute-done.panel_hbm), custom_call_target="tpu_custom_call" | custom-call | flops 1610612736 | bytes 4718592 | tf_op jit(solution)/shard_map/tiles_3_2_1_0/pallas_call | solution.py:81
  42.7 0.0 collective-permute-done.12.refs_4_
  42.7 2.0 %collective-permute-start.3 = (f32[64,512]{1,0:T(8,128)S(1)}, f32[64,512]{1,0:T(8,128)S(1)}, u32[]{:S(2)}, u32[]{:S(2)}) collective-permute-start(f32[64,512]{1,0:T(8,128)S(1)} %get-tuple-element.22), channel_id=1, source_target_pairs={{0,6},{1,7},{2,4},{3,5},{4,2},{5,3},{6,0},{7,1},{8,14},{9,15},{10,... | collective-permute-start | bytes 393224 | tf_op jit(solution)/shard_map/ppermute | solution.py:31
  44.7 0.0 collective-permute-done.13.refs_5_
  44.7 2.8 %collective-permute-start.4 = (f32[64,512]{1,0:T(8,128)S(1)}, f32[64,512]{1,0:T(8,128)S(1)}, u32[]{:S(2)}, u32[]{:S(2)}) collective-permute-start(f32[64,512]{1,0:T(8,128)S(1)} %get-tuple-element.23), channel_id=1, source_target_pairs={{0,7},{1,6},{2,5},{3,4},{4,3},{5,2},{6,1},{7,0},{8,15},{9,14},{10,... | collective-permute-start | bytes 393224 | tf_op jit(solution)/shard_map/ppermute | solution.py:31
  47.5 0.0 collective-permute-done.14.refs_6_
  47.5 0.0 collective-permute-start.5
  47.5 0.0 collective-permute-done.1.refs_0_
  47.5 2.0 %collective-permute-start.6 = (f32[64,512]{1,0:T(8,128)S(1)}, f32[64,512]{1,0:T(8,128)S(1)}, u32[]{:S(2)}, u32[]{:S(2)}) collective-permute-start(f32[64,512]{1,0:T(8,128)S(1)} %get-tuple-element.25), channel_id=1, source_target_pairs={{0,2},{1,3},{2,0},{3,1},{4,6},{5,7},{6,4},{7,5},{8,10},{9,11},{10,... | collective-permute-start | bytes 393224 | tf_op jit(solution)/shard_map/ppermute | solution.py:31
  49.5 5.8 %collective-permute-done.2.refs_1_ = f32[64,512]{1,0:T(8,128)S(1)} collective-permute-done((f32[64,512]{1,0:T(8,128)S(1)}, f32[64,512]{1,0:T(8,128)S(1)}, u32[]{:S(2)}, u32[]{:S(2)}) %collective-permute-start.2) | collective-permute-done | bytes 131104 | tf_op jit(solution)/shard_map/ppermute | solution.py:31
  55.3 0.7 %collective-permute-start.7 = (f32[64,512]{1,0:T(8,128)S(1)}, f32[64,512]{1,0:T(8,128)S(1)}, u32[]{:S(2)}, u32[]{:S(2)}) collective-permute-start(f32[64,512]{1,0:T(8,128)S(1)} %get-tuple-element.26), channel_id=1, source_target_pairs={{0,1},{1,0},{2,3},{3,2},{4,5},{5,4},{6,7},{7,6},{8,9},{9,8},{10,11... | collective-permute-start | bytes 393224 | tf_op jit(solution)/shard_map/ppermute | solution.py:31
  56.0 0.0 copy-done.3
  56.0 1.3 %combine.2.refs_9_ = f32[8,64,1024]{2,1,0:T(8,128)} custom-call(f32[64,512]{1,0:T(8,128)S(1)} %collective-permute-done.8.refs_0_, f32[64,512]{1,0:T(8,128)S(1)} %collective-permute-done.9.refs_1_, f32[64,512]{1,0:T(8,128)S(1)} %collective-permute-done.10.refs_2_, f32[64,512]{1,0:T(8,128)S(1)} %collective-permute-done.11.refs_3_, ...), custom_call_target="tpu_custom_call" | custom-call | flops 262144 | bytes 3145728 | tf_op jit(solution)/shard_map/combine/pallas_call | solution.py:128
  57.3 0.0 collective-permute-done.3.refs_2_
  57.3 0.0 collective-permute-done.4.refs_3_
  57.3 0.1 collective-permute-done.5.refs_4_
  57.4 2.0 %collective-permute-done.6.refs_5_ = f32[64,512]{1,0:T(8,128)S(1)} collective-permute-done((f32[64,512]{1,0:T(8,128)S(1)}, f32[64,512]{1,0:T(8,128)S(1)}, u32[]{:S(2)}, u32[]{:S(2)}) %collective-permute-start.6) | collective-permute-done | bytes 131104 | tf_op jit(solution)/shard_map/ppermute | solution.py:31
  59.4 0.8 %collective-permute-done.7.refs_6_ = f32[64,512]{1,0:T(8,128)S(1)} collective-permute-done((f32[64,512]{1,0:T(8,128)S(1)}, f32[64,512]{1,0:T(8,128)S(1)}, u32[]{:S(2)}, u32[]{:S(2)}) %collective-permute-start.7) | collective-permute-done | bytes 131104 | tf_op jit(solution)/shard_map/ppermute | solution.py:31
  60.2 1.3 %combine.3 = f32[8,64,1024]{2,1,0:T(8,128)} custom-call(f32[64,512]{1,0:T(8,128)S(1)} %collective-permute-done.1.refs_0_, f32[64,512]{1,0:T(8,128)S(1)} %collective-permute-done.2.refs_1_, f32[64,512]{1,0:T(8,128)S(1)} %collective-permute-done.3.refs_2_, f32[64,512]{1,0:T(8,128)S(1)} %collective-permute-done.4.refs_3_, ...), custom_call_target="tpu_custom_call", output_to_operand_aliasing={{}: (9, {})} | custom-call | flops 262144 | bytes 3145728 | tf_op jit(solution)/shard_map/combine/pallas_call | solution.py:128
Async XLA Ops:
  0.0 26.3 %collective-permute-start = (f32[512,1024]{1,0:T(8,128)}, f32[512,1024]{1,0:T(8,128)S(1)}, u32[]{:S(2)}, u32[]{:S(2)}) collective-permute-start(f32[512,1024]{1,0:T(8,128)} %panel_hbm.5), channel_id=1, source_target_pairs={{0,8},{8,16},{16,24},{24,0},{1,9},{9,17},{17,25},{25,1},{2,10},{10... | collective-permute-start | bytes 6291464 | tf_op jit(solution)/shard_map/ppermute | solution.py:150
  0.5 1.6 %copy-start = (f32[512,1024]{1,0:T(8,128)S(1)}, f32[512,1024]{1,0:T(8,128)}, u32[]{:S(2)}) copy-start(f32[512,1024]{1,0:T(8,128)} %x_hbm.9) | copy-start | bytes 6291460
  2.0 1.6 %copy-start.1 = (f32[512,1024]{1,0:T(8,128)S(1)}, f32[512,1024]{1,0:T(8,128)}, u32[]{:S(2)}) copy-start(f32[512,1024]{1,0:T(8,128)} %z_hbm.9) | copy-start | bytes 6291460
  3.6 1.6 %copy-start.2 = (f32[512,1024]{1,0:T(8,128)S(1)}, f32[512,1024]{1,0:T(8,128)}, u32[]{:S(2)}) copy-start(f32[512,1024]{1,0:T(8,128)} %panel_hbm.5) | copy-start | bytes 6291460
  5.2 0.7 %copy-start.4 = (s32[1,1,8]{2,1,0:T(1,128)S(1)}, s32[1,1,8]{2,1,0:T(1,128)}, u32[]{:S(2)}) copy-start(s32[1,1,8]{2,1,0:T(1,128)} %owner.9) | copy-start | bytes 100
  7.9 25.0 %collective-permute-start.8 = (f32[64,512]{1,0:T(8,128)S(1)}, f32[64,512]{1,0:T(8,128)S(1)}, u32[]{:S(2)}, u32[]{:S(2)}) collective-permute-start(f32[64,512]{1,0:T(8,128)S(1)} %tiles_4.1), channel_id=1, source_target_pairs={{0,4},{1,5},{2,6},{3,7},{4,0},{5,1},{6,2},{7,3},{8,12},{9,13},{10,... | collective-permute-start | bytes 393224 | tf_op jit(solution)/shard_map/ppermute | solution.py:31
  14.2 19.2 %collective-permute-start.9 = (f32[64,512]{1,0:T(8,128)S(1)}, f32[64,512]{1,0:T(8,128)S(1)}, u32[]{:S(2)}, u32[]{:S(2)}) collective-permute-start(f32[64,512]{1,0:T(8,128)S(1)} %get-tuple-element.28), channel_id=1, source_target_pairs={{0,5},{1,4},{2,7},{3,6},{4,1},{5,0},{6,3},{7,2},{8,13},{9,12},{10,... | collective-permute-start | bytes 393224 | tf_op jit(solution)/shard_map/ppermute | solution.py:31
  15.5 18.0 %collective-permute-start.10 = (f32[64,512]{1,0:T(8,128)S(1)}, f32[64,512]{1,0:T(8,128)S(1)}, u32[]{:S(2)}, u32[]{:S(2)}) collective-permute-start(f32[64,512]{1,0:T(8,128)S(1)} %get-tuple-element.29), channel_id=1, source_target_pairs={{0,6},{1,7},{2,4},{3,5},{4,2},{5,3},{6,0},{7,1},{8,14},{9,15},{10,... | collective-permute-start | bytes 393224 | tf_op jit(solution)/shard_map/ppermute | solution.py:31
  19.1 17.4 %collective-permute-start.11 = (f32[64,512]{1,0:T(8,128)S(1)}, f32[64,512]{1,0:T(8,128)S(1)}, u32[]{:S(2)}, u32[]{:S(2)}) collective-permute-start(f32[64,512]{1,0:T(8,128)S(1)} %get-tuple-element.30), channel_id=1, source_target_pairs={{0,7},{1,6},{2,5},{3,4},{4,3},{5,2},{6,1},{7,0},{8,15},{9,14},{10,... | collective-permute-start | bytes 393224 | tf_op jit(solution)/shard_map/ppermute | solution.py:31
  26.3 16.3 %collective-permute-start.12 = (f32[64,512]{1,0:T(8,128)S(1)}, f32[64,512]{1,0:T(8,128)S(1)}, u32[]{:S(2)}, u32[]{:S(2)}) collective-permute-start(f32[64,512]{1,0:T(8,128)S(1)} %get-tuple-element.31), channel_id=1, source_target_pairs={{0,3},{1,2},{2,1},{3,0},{4,7},{5,6},{6,5},{7,4},{8,11},{9,10},{10,... | collective-permute-start | bytes 393224 | tf_op jit(solution)/shard_map/ppermute | solution.py:31
  32.9 11.8 %collective-permute-start.13 = (f32[64,512]{1,0:T(8,128)S(1)}, f32[64,512]{1,0:T(8,128)S(1)}, u32[]{:S(2)}, u32[]{:S(2)}) collective-permute-start(f32[64,512]{1,0:T(8,128)S(1)} %get-tuple-element.32), channel_id=1, source_target_pairs={{0,2},{1,3},{2,0},{3,1},{4,6},{5,7},{6,4},{7,5},{8,10},{9,11},{10,... | collective-permute-start | bytes 393224 | tf_op jit(solution)/shard_map/ppermute | solution.py:31
  33.4 14.1 %collective-permute-start.14 = (f32[64,512]{1,0:T(8,128)S(1)}, f32[64,512]{1,0:T(8,128)S(1)}, u32[]{:S(2)}, u32[]{:S(2)}) collective-permute-start(f32[64,512]{1,0:T(8,128)S(1)} %get-tuple-element.33), channel_id=1, source_target_pairs={{0,1},{1,0},{2,3},{3,2},{4,5},{5,4},{6,7},{7,6},{8,9},{9,8},{10,11... | collective-permute-start | bytes 393224 | tf_op jit(solution)/shard_map/ppermute | solution.py:31
  33.6 13.9 %collective-permute-start.1 = (f32[64,512]{1,0:T(8,128)S(1)}, f32[64,512]{1,0:T(8,128)S(1)}, u32[]{:S(2)}, u32[]{:S(2)}) collective-permute-start(f32[64,512]{1,0:T(8,128)S(1)} %get-tuple-element.20), channel_id=1, source_target_pairs={{0,4},{1,5},{2,6},{3,7},{4,0},{5,1},{6,2},{7,3},{8,12},{9,13},{10,... | collective-permute-start | bytes 393224 | tf_op jit(solution)/shard_map/ppermute | solution.py:31
  36.5 19.5 %copy-start.3 = (f32[1,1,8,64,1024]{4,3,2,1,0:T(8,128)S(1)}, f32[1,1,8,64,1024]{4,3,2,1,0:T(8,128)}, u32[]{:S(2)}) copy-start(f32[1,1,8,64,1024]{4,3,2,1,0:T(8,128)} %param.9) | copy-start | bytes 6291460
  36.5 18.7 %collective-permute-start.2 = (f32[64,512]{1,0:T(8,128)S(1)}, f32[64,512]{1,0:T(8,128)S(1)}, u32[]{:S(2)}, u32[]{:S(2)}) collective-permute-start(f32[64,512]{1,0:T(8,128)S(1)} %get-tuple-element.21), channel_id=1, source_target_pairs={{0,5},{1,4},{2,7},{3,6},{4,1},{5,0},{6,3},{7,2},{8,13},{9,12},{10,... | collective-permute-start | bytes 393224 | tf_op jit(solution)/shard_map/ppermute | solution.py:31
  42.7 14.6 %collective-permute-start.3 = (f32[64,512]{1,0:T(8,128)S(1)}, f32[64,512]{1,0:T(8,128)S(1)}, u32[]{:S(2)}, u32[]{:S(2)}) collective-permute-start(f32[64,512]{1,0:T(8,128)S(1)} %get-tuple-element.22), channel_id=1, source_target_pairs={{0,6},{1,7},{2,4},{3,5},{4,2},{5,3},{6,0},{7,1},{8,14},{9,15},{10,... | collective-permute-start | bytes 393224 | tf_op jit(solution)/shard_map/ppermute | solution.py:31
  44.7 12.6 %collective-permute-start.4 = (f32[64,512]{1,0:T(8,128)S(1)}, f32[64,512]{1,0:T(8,128)S(1)}, u32[]{:S(2)}, u32[]{:S(2)}) collective-permute-start(f32[64,512]{1,0:T(8,128)S(1)} %get-tuple-element.23), channel_id=1, source_target_pairs={{0,7},{1,6},{2,5},{3,4},{4,3},{5,2},{6,1},{7,0},{8,15},{9,14},{10,... | collective-permute-start | bytes 393224 | tf_op jit(solution)/shard_map/ppermute | solution.py:31
  47.5 9.9 %collective-permute-start.5 = (f32[64,512]{1,0:T(8,128)S(1)}, f32[64,512]{1,0:T(8,128)S(1)}, u32[]{:S(2)}, u32[]{:S(2)}) collective-permute-start(f32[64,512]{1,0:T(8,128)S(1)} %get-tuple-element.24), channel_id=1, source_target_pairs={{0,3},{1,2},{2,1},{3,0},{4,7},{5,6},{6,5},{7,4},{8,11},{9,10},{10,... | collective-permute-start | bytes 393224 | tf_op jit(solution)/shard_map/ppermute | solution.py:31
  47.5 11.9 %collective-permute-start.6 = (f32[64,512]{1,0:T(8,128)S(1)}, f32[64,512]{1,0:T(8,128)S(1)}, u32[]{:S(2)}, u32[]{:S(2)}) collective-permute-start(f32[64,512]{1,0:T(8,128)S(1)} %get-tuple-element.25), channel_id=1, source_target_pairs={{0,2},{1,3},{2,0},{3,1},{4,6},{5,7},{6,4},{7,5},{8,10},{9,11},{10,... | collective-permute-start | bytes 393224 | tf_op jit(solution)/shard_map/ppermute | solution.py:31
  55.3 5.0 %collective-permute-start.7 = (f32[64,512]{1,0:T(8,128)S(1)}, f32[64,512]{1,0:T(8,128)S(1)}, u32[]{:S(2)}, u32[]{:S(2)}) collective-permute-start(f32[64,512]{1,0:T(8,128)S(1)} %get-tuple-element.26), channel_id=1, source_target_pairs={{0,1},{1,0},{2,3},{3,2},{4,5},{5,4},{6,7},{7,6},{8,9},{9,8},{10,11... | collective-permute-start | bytes 393224 | tf_op jit(solution)/shard_map/ppermute | solution.py:31

commit v2 on v0

v2 whole, which is shorter than its diff:
```python
import functools

import jax
import jax.numpy as jnp
from jax import lax
from jax.experimental import pallas as pl
from jax.experimental.pallas import tpu as pltpu
from jax.sharding import PartitionSpec as P

PARTS = 2
NT = (((1,), (1,)), ((), ()))
HBM = pl.BlockSpec(memory_space=pltpu.HBM)
VMEM = pl.BlockSpec(memory_space=pltpu.VMEM)
F32 = jnp.float32
BF16 = jnp.bfloat16


def exchange(piece, j, groups):
    return lax.ppermute(piece, "grid", [(i, i ^ j) for i in range(groups)])


def split(x):
    high = x.astype(BF16)
    return high, (x - high.astype(F32)).astype(BF16)


def dot(a, b):
    return lax.dot_general(a, b, NT, preferred_element_type=F32)


def products(rows_hi, rows_lo, panel_hi, panel_lo):
    return dot(rows_hi, panel_hi) + (dot(rows_lo, panel_hi) + dot(rows_hi, panel_lo))


def row_copies(js, groups, owner, x_hbm, z_hbm, rows, sems, base=0):
    tile = x_hbm.shape[0] // groups
    me = lax.axis_index("grid")
    copies = []
    for i, j in enumerate(js):
        to = me ^ j
        t = jnp.int32(0)
        for k in range(groups):
            t = t + jnp.where(owner[0, 0, k] == to, k, 0)
        at = pl.ds(pl.multiple_of(t * tile, tile), tile)
        place = pl.ds((base + i) * tile, tile)
        for s, hbm in enumerate((x_hbm, z_hbm)):
            copies.append(pltpu.make_async_copy(hbm.at[at], rows.at[s, place], sems.at[s, base + i]))
    return copies


def write_pieces(pieces, start, both):
    tile, cols = pieces[0].shape[1], both.shape[1]
    count = both.shape[0] // 2
    at = 0
    for piece in pieces:
        for c in range(piece.shape[0]):
            piece[c, :, start : start + cols] = both[at : at + tile] * both[count + at : count + at + tile]
            at += tile


def first_kernel(js, groups, owner_hbm, x_hbm, z_hbm, panel_hbm, *refs):
    piece, rows, hi, lo, panel, owner, owner_sem, row_sems, panel_sems = refs
    used = piece.shape[0] * piece.shape[1]
    part = panel_hbm.shape[0] // PARTS
    fetch_owner = pltpu.make_async_copy(owner_hbm, owner, owner_sem)
    fetch_owner.start()
    spans = [slice(h * part, (h + 1) * part) for h in range(PARTS)]
    fetches = []
    for h, at in enumerate(spans):
        fetches.append(pltpu.make_async_copy(panel_hbm.at[at], panel.at[at], panel_sems.at[h]))
        fetches[h].start()
    fetch_owner.wait()
    copies = row_copies(js, groups, owner, x_hbm, z_hbm, rows, row_sems)
    for copy in copies:
        copy.start()
    for h, at in enumerate(spans):
        fetches[h].wait()
        hi[at, :], lo[at, :] = split(panel[at, :])
    ready = 2 * piece.shape[0]
    for copy in copies[:ready]:
        copy.wait()
    own_hi, own_lo = split(jnp.concatenate([rows[0, :used], rows[1, :used]], axis=0))
    write_pieces([piece], 0, products(own_hi, own_lo, hi[...], lo[...]))
    for copy in copies[ready:]:
        copy.wait()


def first(js, count, groups, owner, times_x, times_zinv, panel):
    rows, width = times_x.shape
    tile, cols, n = rows // groups, panel.shape[0], len(js)
    shape = jax.ShapeDtypeStruct
    return pl.pallas_call(
        functools.partial(first_kernel, js, groups),
        out_shape=[
            shape((count, tile, cols), F32),
            shape((2, n * tile, width), F32),
            shape((cols, width), BF16),
            shape((cols, width), BF16),
        ],
        in_specs=[HBM] * 4,
        out_specs=[VMEM] * 4,
        scratch_shapes=[
            pltpu.VMEM(panel.shape, F32),
            pltpu.SMEM(owner.shape, owner.dtype),
            pltpu.SemaphoreType.DMA,
            pltpu.SemaphoreType.DMA((2, n)),
            pltpu.SemaphoreType.DMA((PARTS,)),
        ],
        compiler_params=pltpu.CompilerParams(vmem_limit_bytes=24 << 20),
        cost_estimate=pl.CostEstimate(
            flops=12 * count * tile * cols * width,
            bytes_accessed=4 * (2 * n * tile * width + cols * width),
            transcendentals=0,
        ),
        name="first",
    )(owner, times_x, times_zinv, panel)


def second_kernel(skip, js, groups, n_far, owner_hbm, x_hbm, z_hbm, rows, hi, lo, *refs):
    pieces, (more_rows, owner, owner_sem, row_sems) = refs[:-4], refs[-4:]
    fetch_owner = pltpu.make_async_copy(owner_hbm, owner, owner_sem)
    fetch_owner.start()
    tile = pieces[0].shape[1]

    def far_pieces(some, at):
        at = slice(at * tile, (at + len(some)) * tile)
        own_hi, own_lo = split(jnp.concatenate([rows[0, at], rows[1, at]], axis=0))
        write_pieces(some, 0, products(own_hi, own_lo, hi[...], lo[...]))

    far_pieces(pieces[:1], skip)
    fetch_owner.wait()
    copies = row_copies(js, groups, owner, x_hbm, z_hbm, more_rows, row_sems)
    for copy in copies:
        copy.start()
    far_pieces(pieces[1:n_far], skip + 1)
    for copy in copies:
        copy.wait()
    own_hi, own_lo = split(jnp.concatenate([more_rows[0], more_rows[1]], axis=0))
    write_pieces(pieces[n_far:], 0, products(own_hi, own_lo, hi[...], lo[...]))


def second(rows, panel, skip, far_counts, near_counts, js, tile, groups, owner, times_x, times_zinv):
    width, cols, n = rows.shape[2], panel[0].shape[0], sum(far_counts + near_counts)
    shape = jax.ShapeDtypeStruct
    out_shape = [shape((c, tile, cols), F32) for c in far_counts + near_counts]
    out_shape.append(shape((2, len(js) * tile, width), F32))
    return pl.pallas_call(
        functools.partial(second_kernel, skip, js, groups, len(far_counts)),
        out_shape=out_shape,
        in_specs=[HBM] * 3 + [VMEM] * 3,
        out_specs=[VMEM] * len(out_shape),
        scratch_shapes=[
            pltpu.SMEM(owner.shape, owner.dtype),
            pltpu.SemaphoreType.DMA,
            pltpu.SemaphoreType.DMA((2, len(js))),
        ],
        compiler_params=pltpu.CompilerParams(vmem_limit_bytes=24 << 20),
        cost_estimate=pl.CostEstimate(
            flops=12 * n * tile * cols * width,
            bytes_accessed=4 * (2 * n * tile * width + cols * width),
            transcendentals=0,
        ),
        name="second",
    )(owner, times_x, times_zinv, rows, *panel)


def more_kernel(skip, rows, panel, *pieces):
    tile = pieces[0].shape[1]
    at = slice(skip * tile, (skip + sum(p.shape[0] for p in pieces)) * tile)
    own_hi, own_lo = split(jnp.concatenate([rows[0, at], rows[1, at]], axis=0))
    write_pieces(pieces, 0, products(own_hi, own_lo, *split(panel[...])))


def more(name, rows, panel, skip, counts, tile):
    width, cols, n = rows.shape[2], panel.shape[0], sum(counts)
    return pl.pallas_call(
        functools.partial(more_kernel, skip),
        out_shape=[jax.ShapeDtypeStruct((c, tile, cols), F32) for c in counts],
        in_specs=[VMEM] * 2,
        out_specs=[VMEM] * len(counts),
        compiler_params=pltpu.CompilerParams(vmem_limit_bytes=24 << 20),
        cost_estimate=pl.CostEstimate(
            flops=12 * n * tile * cols * width,
            bytes_accessed=4 * (2 * n * tile * width + cols * width),
            transcendentals=0,
        ),
        name=name,
    )(rows, panel)


def combine_kernel(places, begun, n, *refs):
    arrays, update = refs[:n], refs[n]
    out, buf, sem = refs[n + (2 if begun else 1) :]
    me = lax.axis_index("grid")
    cols = arrays[0].shape[2]
    stores = []
    for i, (j, start) in enumerate(places):
        buf[i] = arrays[i][0] - update[me ^ j, :, start : start + cols]
        at = (me ^ j, slice(None), pl.ds(start, cols))
        stores.append(pltpu.make_async_copy(buf.at[i], out.at[at], sem.at[i]))
        stores[i].start()
    for copy in stores:
        copy.wait()


def combine(arrays, places, update, out):
    n = len(arrays)
    tile = arrays[0].shape[1:]
    operands = list(arrays) + [update] + ([] if out is None else [out])
    size = n * tile[0] * tile[1]
    return pl.pallas_call(
        functools.partial(combine_kernel, tuple(places), out is not None, n),
        out_shape=jax.ShapeDtypeStruct(update.shape, update.dtype),
        in_specs=[VMEM] * (n + 1) + [HBM] * (len(operands) - n - 1),
        out_specs=HBM,
        scratch_shapes=[pltpu.VMEM((n, *tile), F32), pltpu.SemaphoreType.DMA((n,))],
        input_output_aliases={} if out is None else {n + 1: 0},
        compiler_params=pltpu.CompilerParams(vmem_limit_bytes=16 << 20),
        cost_estimate=pl.CostEstimate(flops=size, bytes_accessed=12 * size, transcendentals=0),
        name="combine",
    )(*operands)


def after(value, *earlier):
    return lax.optimization_barrier((value, *earlier))[0] if earlier else value


def from_behind(array, axis, by):
    length = lax.axis_size(axis)
    return lax.ppermute(array, axis, [(i, (i + by) % length) for i in range(length)])


def body(constraints, times_x, times_zinv, owner, update):
    groups = lax.axis_size("grid")
    tile = times_x.shape[0] // groups
    cols = constraints.shape[0]
    update = update[0, 0]
    times_x, times_zinv, panel, owner = (
        pltpu.with_memory_space_constraint(a, pltpu.HBM) for a in (times_x, times_zinv, constraints, owner)
    )
    half = groups // 2
    far = tuple(range(half, groups))
    near = (*range(2, half), 1, 0)
    ones = (1,) * half

    moved = from_behind(constraints, "blk", 1)
    piece, far_rows, *panel = first(far, 1, groups, owner, times_x, times_zinv, panel)
    *pieces, near_rows = second(
        far_rows, panel, 1, ones[1:], ones, near, tile, groups, owner, times_x, times_zinv
    )
    ready = dict(zip([(j, 0) for j in far + near], [piece, *pieces]))
    got = {}

    def send(*keys):
        for key in keys:
            got[key] = exchange(ready[key], key[0], groups) if key[0] else ready[key]

    a, a2, n, n2 = ([(j, step) for j in some] for some in (far, near[:-1]) for step in range(2))
    own, own2 = (0, 0), (0, 1)
    send(*ready)
    moved = after(moved, *[got[key] for key in a[:2] + n[:1]])
    ready.update(zip(a2[:1], more("more_first", far_rows, moved, 0, (1,), tile)))
    ready.update(zip(a2[1:], more("more_far", far_rows, moved, 1, ones[1:], tile)))
    ready.update(zip([*n2, own2], more("more_near", near_rows, moved, 0, ones, tile)))
    send(*a2, *n2, own2)
    out = None
    for keys in ([own, *a[:2], *n[:1], *a[2:], *n[1:]], [own2, *a2[:-1], *n2[:1]], [*n2[1:2], a2[-1], *n2[2:]]):
        out = combine([got[key] for key in keys], [(j, step * cols) for j, step in keys], update, out)
    return out[None, None]


def solution(mesh):
    placed = (
        P(("blk", "grid"), None),
        P(("blk", "grid"), None),
        P(("blk", "grid"), None),
        P("blk", "grid", None),
        P("blk", "grid", None, None, None),
    )
    return jax.shard_map(
        body,
        mesh=mesh,
        in_specs=placed,
        out_specs=P("blk", "grid", None, None, None),
        check_vma=False,
    )
```

time: 83.4 us -> 57.4 us (0.69)
  blocking collectives: 29.7 us -> 0 us
  starting transfers between devices: 7.71 us -> 30.7 us
  matrix products: 22.3 us -> 0 us
  Pallas kernels: 0 us -> 15.6 us
  local copies, waits for them, and re-layouts: 5.76 us -> 0.01 us
  waiting for transfers between devices: 14.9 us -> 10.4 us
  other arithmetic: 2.68 us -> 0 us
    ppermute x0 -> x14, starting transfers between devices: none -> 30.2 us  [exchange(): return lax.ppermute(piece, 'grid', [(i, i ^ j) for i in range(groups)])]
    all_to_all x1 -> x0, blocking collectives: 29.7 us -> none  [body(): lax.all_to_all(block, 'grid', split_axis=0, concat_axis=0, tiled=True)]
    dot_general x4 -> x0, matrix products: 22.3 us -> none  [the longest x2 12 us: hadamard_panel(): jnp.dot(rows_x, panel.T, preferred_element_type=jnp.float32, precision=la...]
    pallas_call x0 -> x8, Pallas kernels: none -> 15.6 us  [the longest x1 5.21 us: second(): pl.pallas_call(functools.partial(second_kernel, skip, js, groups, len(far...]
    all_to_all x1 -> x0, waiting for transfers between devices: 13.3 us -> none  [body(): lax.all_to_all(block, 'grid', split_axis=0, concat_axis=0, tiled=True)]
    ppermute x0 -> x14, waiting for transfers between devices: none -> 8.98 us  [exchange(): return lax.ppermute(piece, 'grid', [(i, i ^ j) for i in range(groups)])]
    all_to_all x1 -> x0, starting transfers between devices: 7.26 us -> none  [body(): lax.all_to_all(block, 'grid', split_axis=0, concat_axis=0, tiled=True)]
    gather x2 -> x0, local copies, waits for them, and re-layouts: 5.57 us -> none  [the longest x1 3.57 us: body(): times_x.reshape(groups, tile_rows, width)[inverse].reshape(row_count, width)]
  transfers between devices with their start and end apart: 2 -> 15, of which waited for: 2 -> 7; matrix products, arithmetic and copies ran while one was open for 35% -> 0% of each run, Pallas kernels for 0% -> 26%
where the time goes in v2:
time: 57.4 us; the launch traced here: 56.8 us
  starting transfers between devices  30.7 us (53%)
  Pallas kernels  15.6 us (27%)
  waiting for transfers between devices  10.4 us (18%)
    ppermute x14, starting transfers between devices, exchange(): return lax.ppermute(piece, 'grid', [(i, i ^ j) for i in range(groups)])  30.2 us
    ppermute x14, waiting for transfers between devices, exchange(): return lax.ppermute(piece, 'grid', [(i, i ^ j) for i in range(groups)])  8.98 us
    pallas_call x1, Pallas kernels, second(): pl.pallas_call(functools.partial(second_kernel, skip, js, groups, len(far...  5.21 us
    pallas_call x3, Pallas kernels, more(): pl.pallas_call(functools.partial(more_kernel, skip), out_shape=[jax.Shape...  4.41 us
    pallas_call x1, Pallas kernels, first(): pl.pallas_call(functools.partial(first_kernel, js, groups), out_shape=[sh...  3.27 us
    pallas_call x3, Pallas kernels, combine(): pl.pallas_call(functools.partial(combine_kernel, tuple(places), out is no...  2.71 us
    ppermute x1, waiting for transfers between devices, from_behind(): lax.ppermute(array, axis, [(i, (i + by) % length) for i in range(length)])  1.43 us
  transfers between devices with their start and end apart: 15, of which 7 were waited for; matrix products, arithmetic and copies ran while one was open for 0% of the time, Pallas kernels for 26%

profile of v2, /device:TPU:0, one launch (start us, length us, event | category | flops | bytes accessed | tf_op | source)
XLA Modules:
  0.0 56.8 jit_solution(7691925805257078909)
XLA Ops:
  0.0 0.5 collective-permute-start
  0.5 3.3 %first.1 = (f32[1,64,512]{2,1,0:T(8,128)S(1)}, f32[2,256,1024]{2,1,0:T(8,128)S(1)}, bf16[512,1024]{1,0:T(8,128)(2,1)S(1)}, bf16[512,1024]{1,0:T(8,128)(2,1)S(1)}) custom-call(s32[1,1,8]{2,1,0:T(1,128)} %owner_hbm.3, f32[512,1024]{1,0:T(8,128)} %x_hbm.3, f32[512,1024]{1,0:T(8,128)} %z_hbm.3, f32[512,1024]{1,0:T(8,128)} %panel_hbm.1), custom_call_target="tpu_custom_call" | custom-call | flops 402653184 | bytes 4194304 | tf_op jit(solution)/shard_map/first/pallas_call | solution.py:92
  3.7 3.7 %collective-permute-start.1 = (f32[1,64,512]{2,1,0:T(8,128)S(1)}, f32[1,64,512]{2,1,0:T(8,128)S(1)}, u32[]{:S(2)}, u32[]{:S(2)}) collective-permute-start(f32[1,64,512]{2,1,0:T(8,128)S(1)} %get-tuple-element.29), channel_id=1, source_target_pairs={{0,4},{1,5},{2,6},{3,7},{4,0},{5,1},{6,2},{7,3},{8,12},{9,13},{10,... | collective-permute-start | bytes 393224 | tf_op jit(solution)/shard_map/ppermute | solution.py:19
  7.4 5.2 %second.1 = (f32[1,64,512]{2,1,0:T(8,128)S(1)}, f32[1,64,512]{2,1,0:T(8,128)S(1)}, f32[1,64,512]{2,1,0:T(8,128)S(1)}, f32[1,64,512]{2,1,0:T(8,128)S(1)}, f32[1,6...) custom-call(s32[1,1,8]{2,1,0:T(1,128)} %owner_hbm.3, ...), custom_call_target="tpu_custom_call" | custom-call | flops 2818572288 | bytes 5767168 | tf_op jit(solution)/shard_map/second/pallas_call | solution.py:147
  12.6 1.3 %collective-permute-start.2 = (f32[1,64,512]{2,1,0:T(8,128)S(1)}, f32[1,64,512]{2,1,0:T(8,128)S(1)}, u32[]{:S(2)}, u32[]{:S(2)}) collective-permute-start(f32[1,64,512]{2,1,0:T(8,128)S(1)} %get-tuple-element.30), channel_id=1, source_target_pairs={{0,5},{1,4},{2,7},{3,6},{4,1},{5,0},{6,3},{7,2},{8,13},{9,12},{10,... | collective-permute-start | bytes 393224 | tf_op jit(solution)/shard_map/ppermute | solution.py:19
  13.9 1.6 %collective-permute-start.3 = (f32[1,64,512]{2,1,0:T(8,128)S(1)}, f32[1,64,512]{2,1,0:T(8,128)S(1)}, u32[]{:S(2)}, u32[]{:S(2)}) collective-permute-start(f32[1,64,512]{2,1,0:T(8,128)S(1)} %get-tuple-element.31), channel_id=1, source_target_pairs={{0,2},{1,3},{2,0},{3,1},{4,6},{5,7},{6,4},{7,5},{8,10},{9,11},{10,... | collective-permute-start | bytes 393224 | tf_op jit(solution)/shard_map/ppermute | solution.py:19
  15.5 2.5 %collective-permute-start.11 = (f32[1,64,512]{2,1,0:T(8,128)S(1)}, f32[1,64,512]{2,1,0:T(8,128)S(1)}, u32[]{:S(2)}, u32[]{:S(2)}) collective-permute-start(f32[1,64,512]{2,1,0:T(8,128)S(1)} %get-tuple-element.41), channel_id=1, source_target_pairs={{0,6},{1,7},{2,4},{3,5},{4,2},{5,3},{6,0},{7,1},{8,14},{9,15},{10,... | collective-permute-start | bytes 393224 | tf_op jit(solution)/shard_map/ppermute | solution.py:19
  18.0 0.0 collective-permute-done.1.refs_1_
  18.0 3.6 %collective-permute-start.12 = (f32[1,64,512]{2,1,0:T(8,128)S(1)}, f32[1,64,512]{2,1,0:T(8,128)S(1)}, u32[]{:S(2)}, u32[]{:S(2)}) collective-permute-start(f32[1,64,512]{2,1,0:T(8,128)S(1)} %get-tuple-element.42), channel_id=1, source_target_pairs={{0,7},{1,6},{2,5},{3,4},{4,3},{5,2},{6,1},{7,0},{8,15},{9,14},{10,... | collective-permute-start | bytes 393224 | tf_op jit(solution)/shard_map/ppermute | solution.py:19
  21.6 1.8 %collective-permute-done.2.refs_2_ = f32[1,64,512]{2,1,0:T(8,128)S(1)} collective-permute-done((f32[1,64,512]{2,1,0:T(8,128)S(1)}, f32[1,64,512]{2,1,0:T(8,128)S(1)}, u32[]{:S(2)}, u32[]{:S(2)}) %collective-permute-start.2) | collective-permute-done | bytes 131104 | tf_op jit(solution)/shard_map/ppermute | solution.py:19
  23.4 0.0 collective-permute-start.13
  23.4 0.0 collective-permute-done.3.refs_3_
  23.4 1.5 %collective-permute-start.14 = (f32[1,64,512]{2,1,0:T(8,128)S(1)}, f32[1,64,512]{2,1,0:T(8,128)S(1)}, u32[]{:S(2)}, u32[]{:S(2)}) collective-permute-start(f32[1,64,512]{2,1,0:T(8,128)S(1)} %get-tuple-element.44), channel_id=1, source_target_pairs={{0,1},{1,0},{2,3},{3,2},{4,5},{5,4},{6,7},{7,6},{8,9},{9,8},{10,11... | collective-permute-start | bytes 393224 | tf_op jit(solution)/shard_map/ppermute | solution.py:19
  24.9 1.4 %collective-permute-done.panel = f32[512,1024]{1,0:T(8,128)S(1)} collective-permute-done((f32[512,1024]{1,0:T(8,128)}, f32[512,1024]{1,0:T(8,128)S(1)}, u32[]{:S(2)}, u32[]{:S(2)}) %collective-permute-start) | collective-permute-done | bytes 2097184 | tf_op jit(solution)/shard_map/ppermute | solution.py:230
  26.3 1.2 %more_first.1 = f32[1,64,512]{2,1,0:T(8,128)S(1)} custom-call(f32[2,256,1024]{2,1,0:T(8,128)S(1)} %get-tuple-element.25.rows, f32[512,1024]{1,0:T(8,128)S(1)} %collective-permute-done.panel), custom_call_target="tpu_custom_call" | custom-call | flops 402653184 | bytes 2621440 | tf_op jit(solution)/shard_map/more_first/pallas_call | solution.py:176
  27.5 6.0 %collective-permute-start.7 = (f32[1,64,512]{2,1,0:T(8,128)S(1)}, f32[1,64,512]{2,1,0:T(8,128)S(1)}, u32[]{:S(2)}, u32[]{:S(2)}) collective-permute-start(f32[1,64,512]{2,1,0:T(8,128)S(1)} %more_first.1), channel_id=1, source_target_pairs={{0,4},{1,5},{2,6},{3,7},{4,0},{5,1},{6,2},{7,3},{8,12},{9,13},{10,... | collective-permute-start | bytes 393224 | tf_op jit(solution)/shard_map/ppermute | solution.py:19
  33.5 1.4 %more_far.1 = (f32[1,64,512]{2,1,0:T(8,128)S(1)}, f32[1,64,512]{2,1,0:T(8,128)S(1)}, f32[1,64,512]{2,1,0:T(8,128)S(1)}) custom-call(f32[2,256,1024]{2,1,0:T(8,128)S(1)} %get-tuple-element.25.rows, f32[512,1024]{1,0:T(8,128)S(1)} %collective-permute-done.panel), custom_call_target="tpu_custom_call" | custom-call | flops 1207959552 | bytes 3670016 | tf_op jit(solution)/shard_map/more_far/pallas_call | solution.py:176
  34.9 0.0 collective-permute-done.11.refs_4_
  34.9 0.1 collective-permute-start.8
  35.0 0.0 copy-start
  35.0 1.8 %more_near.1 = (f32[1,64,512]{2,1,0:T(8,128)S(1)}, f32[1,64,512]{2,1,0:T(8,128)S(1)}, f32[1,64,512]{2,1,0:T(8,128)S(1)}, f32[1,64,512]{2,1,0:T(8,128)S(1)}) custom-call(f32[2,256,1024]{2,1,0:T(8,128)S(1)} %get-tuple-element.28.rows, f32[512,1024]{1,0:T(8,128)S(1)} %collective-permute-done.panel), custom_call_target="tpu_custom_call" | custom-call | flops 1610612736 | bytes 4194304 | tf_op jit(solution)/shard_map/more_near/pallas_call | solution.py:176
  36.8 0.0 collective-permute-done.12.refs_5_
  36.9 2.2 %collective-permute-start.4 = (f32[1,64,512]{2,1,0:T(8,128)S(1)}, f32[1,64,512]{2,1,0:T(8,128)S(1)}, u32[]{:S(2)}, u32[]{:S(2)}) collective-permute-start(f32[1,64,512]{2,1,0:T(8,128)S(1)} %get-tuple-element.33), channel_id=1, source_target_pairs={{0,3},{1,2},{2,1},{3,0},{4,7},{5,6},{6,5},{7,4},{8,11},{9,10},{10,... | collective-permute-start | bytes 393224 | tf_op jit(solution)/shard_map/ppermute | solution.py:19
  39.1 0.0 collective-permute-done.13.refs_6_
  39.1 5.8 %collective-permute-start.9 = (f32[1,64,512]{2,1,0:T(8,128)S(1)}, f32[1,64,512]{2,1,0:T(8,128)S(1)}, u32[]{:S(2)}, u32[]{:S(2)}) collective-permute-start(f32[1,64,512]{2,1,0:T(8,128)S(1)} %get-tuple-element.38), channel_id=1, source_target_pairs={{0,6},{1,7},{2,4},{3,5},{4,2},{5,3},{6,0},{7,1},{8,14},{9,15},{10,... | collective-permute-start | bytes 393224 | tf_op jit(solution)/shard_map/ppermute | solution.py:19
  44.9 0.0 collective-permute-done.14.refs_7_
  44.9 0.0 collective-permute-start.10
  44.9 0.0 collective-permute-done.7.refs_1_
  44.9 1.1 %collective-permute-start.5 = (f32[1,64,512]{2,1,0:T(8,128)S(1)}, f32[1,64,512]{2,1,0:T(8,128)S(1)}, u32[]{:S(2)}, u32[]{:S(2)}) collective-permute-start(f32[1,64,512]{2,1,0:T(8,128)S(1)} %get-tuple-element.34), channel_id=1, source_target_pairs={{0,7},{1,6},{2,5},{3,4},{4,3},{5,2},{6,1},{7,0},{8,15},{9,14},{10,... | collective-permute-start | bytes 393224 | tf_op jit(solution)/shard_map/ppermute | solution.py:19
  45.9 1.0 %collective-permute-done.8.refs_2_ = f32[1,64,512]{2,1,0:T(8,128)S(1)} collective-permute-done((f32[1,64,512]{2,1,0:T(8,128)S(1)}, f32[1,64,512]{2,1,0:T(8,128)S(1)}, u32[]{:S(2)}, u32[]{:S(2)}) %collective-permute-start.8) | collective-permute-done | bytes 131104 | tf_op jit(solution)/shard_map/ppermute | solution.py:19
  46.9 0.9 %collective-permute-start.6 = (f32[1,64,512]{2,1,0:T(8,128)S(1)}, f32[1,64,512]{2,1,0:T(8,128)S(1)}, u32[]{:S(2)}, u32[]{:S(2)}) collective-permute-start(f32[1,64,512]{2,1,0:T(8,128)S(1)} %get-tuple-element.35), channel_id=1, source_target_pairs={{0,1},{1,0},{2,3},{3,2},{4,5},{5,4},{6,7},{7,6},{8,9},{9,8},{10,11... | collective-permute-start | bytes 393224 | tf_op jit(solution)/shard_map/ppermute | solution.py:19
  47.8 0.0 copy-done
  47.8 1.0 %combine.3.refs_6_ = f32[8,64,1024]{2,1,0:T(8,128)} custom-call(f32[1,64,512]{2,1,0:T(8,128)S(1)} %get-tuple-element.40.refs_0_, f32[1,64,512]{2,1,0:T(8,128)S(1)} %collective-permute-done.1.refs_1_, f32[1,64,512]{2,1,0:T(8,128)S(1)} %collective-permute-done.2.refs_2_, f32[1,64,512]{2,1,0:T(8,128)S(1)} %collective-permute-done.3.refs_3_, ...), custom_call_target="tpu_custom_call" | custom-call | flops 262144 | bytes 3145728 | tf_op jit(solution)/shard_map/combine/pallas_call | solution.py:211
  48.9 3.2 %collective-permute-done.9.refs_3_ = f32[1,64,512]{2,1,0:T(8,128)S(1)} collective-permute-done((f32[1,64,512]{2,1,0:T(8,128)S(1)}, f32[1,64,512]{2,1,0:T(8,128)S(1)}, u32[]{:S(2)}, u32[]{:S(2)}) %collective-permute-start.9) | collective-permute-done | bytes 131104 | tf_op jit(solution)/shard_map/ppermute | solution.py:19
  52.1 0.5 collective-permute-done.10.refs_4_
  52.6 0.9 %combine.4.refs_4_ = f32[8,64,1024]{2,1,0:T(8,128)} custom-call(f32[1,64,512]{2,1,0:T(8,128)S(1)} %get-tuple-element.36.refs_0_, f32[1,64,512]{2,1,0:T(8,128)S(1)} %collective-permute-done.7.refs_1_, f32[1,64,512]{2,1,0:T(8,128)S(1)} %collective-permute-done.8.refs_2_, ...), custom_call_target="tpu_custom_call", output_to_operand_aliasing={{}: (6, {})} | custom-call | flops 163840 | bytes 1966080 | tf_op jit(solution)/shard_map/combine/pallas_call | solution.py:211
  53.5 0.0 collective-permute-done.4.refs_0_
  53.5 0.7 %collective-permute-done.5.refs_1_ = f32[1,64,512]{2,1,0:T(8,128)S(1)} collective-permute-done((f32[1,64,512]{2,1,0:T(8,128)S(1)}, f32[1,64,512]{2,1,0:T(8,128)S(1)}, u32[]{:S(2)}, u32[]{:S(2)}) %collective-permute-start.5) | collective-permute-done | bytes 131104 | tf_op jit(solution)/shard_map/ppermute | solution.py:19
  54.2 1.8 %collective-permute-done.6.refs_2_ = f32[1,64,512]{2,1,0:T(8,128)S(1)} collective-permute-done((f32[1,64,512]{2,1,0:T(8,128)S(1)}, f32[1,64,512]{2,1,0:T(8,128)S(1)}, u32[]{:S(2)}, u32[]{:S(2)}) %collective-permute-start.6) | collective-permute-done | bytes 131104 | tf_op jit(solution)/shard_map/ppermute | solution.py:19
  56.0 0.8 %combine.5 = f32[8,64,1024]{2,1,0:T(8,128)} custom-call(f32[1,64,512]{2,1,0:T(8,128)S(1)} %collective-permute-done.4.refs_0_, f32[1,64,512]{2,1,0:T(8,128)S(1)} %collective-permute-done.5.refs_1_, f32[1,64,512]{2,1,0:T(8,128)S(1)} %collective-permute-done.6.refs_2_, f32[8,64,1024]{2,1,0:T(8,128)S(1)} %bitcast.4, ...), custom_call_target="tpu_custom_call", output_to_operand_aliasing={{}: (4, {})} | custom-call | flops 98304 | bytes 1179648 | tf_op jit(solution)/shard_map/combine/pallas_call | solution.py:211
Async XLA Ops:
  0.0 26.3 %collective-permute-start = (f32[512,1024]{1,0:T(8,128)}, f32[512,1024]{1,0:T(8,128)S(1)}, u32[]{:S(2)}, u32[]{:S(2)}) collective-permute-start(f32[512,1024]{1,0:T(8,128)} %panel_hbm.1), channel_id=1, source_target_pairs={{0,8},{8,16},{16,24},{24,0},{1,9},{9,17},{17,25},{25,1},{2,10},{10... | collective-permute-start | bytes 6291464 | tf_op jit(solution)/shard_map/ppermute | solution.py:230
  3.7 14.3 %collective-permute-start.1 = (f32[1,64,512]{2,1,0:T(8,128)S(1)}, f32[1,64,512]{2,1,0:T(8,128)S(1)}, u32[]{:S(2)}, u32[]{:S(2)}) collective-permute-start(f32[1,64,512]{2,1,0:T(8,128)S(1)} %get-tuple-element.29), channel_id=1, source_target_pairs={{0,4},{1,5},{2,6},{3,7},{4,0},{5,1},{6,2},{7,3},{8,12},{9,13},{10,... | collective-permute-start | bytes 393224 | tf_op jit(solution)/shard_map/ppermute | solution.py:19
  12.6 10.8 %collective-permute-start.2 = (f32[1,64,512]{2,1,0:T(8,128)S(1)}, f32[1,64,512]{2,1,0:T(8,128)S(1)}, u32[]{:S(2)}, u32[]{:S(2)}) collective-permute-start(f32[1,64,512]{2,1,0:T(8,128)S(1)} %get-tuple-element.30), channel_id=1, source_target_pairs={{0,5},{1,4},{2,7},{3,6},{4,1},{5,0},{6,3},{7,2},{8,13},{9,12},{10,... | collective-permute-start | bytes 393224 | tf_op jit(solution)/shard_map/ppermute | solution.py:19
  13.9 9.5 %collective-permute-start.3 = (f32[1,64,512]{2,1,0:T(8,128)S(1)}, f32[1,64,512]{2,1,0:T(8,128)S(1)}, u32[]{:S(2)}, u32[]{:S(2)}) collective-permute-start(f32[1,64,512]{2,1,0:T(8,128)S(1)} %get-tuple-element.31), channel_id=1, source_target_pairs={{0,2},{1,3},{2,0},{3,1},{4,6},{5,7},{6,4},{7,5},{8,10},{9,11},{10,... | collective-permute-start | bytes 393224 | tf_op jit(solution)/shard_map/ppermute | solution.py:19
  15.5 19.4 %collective-permute-start.11 = (f32[1,64,512]{2,1,0:T(8,128)S(1)}, f32[1,64,512]{2,1,0:T(8,128)S(1)}, u32[]{:S(2)}, u32[]{:S(2)}) collective-permute-start(f32[1,64,512]{2,1,0:T(8,128)S(1)} %get-tuple-element.41), channel_id=1, source_target_pairs={{0,6},{1,7},{2,4},{3,5},{4,2},{5,3},{6,0},{7,1},{8,14},{9,15},{10,... | collective-permute-start | bytes 393224 | tf_op jit(solution)/shard_map/ppermute | solution.py:19
  18.0 18.9 %collective-permute-start.12 = (f32[1,64,512]{2,1,0:T(8,128)S(1)}, f32[1,64,512]{2,1,0:T(8,128)S(1)}, u32[]{:S(2)}, u32[]{:S(2)}) collective-permute-start(f32[1,64,512]{2,1,0:T(8,128)S(1)} %get-tuple-element.42), channel_id=1, source_target_pairs={{0,7},{1,6},{2,5},{3,4},{4,3},{5,2},{6,1},{7,0},{8,15},{9,14},{10,... | collective-permute-start | bytes 393224 | tf_op jit(solution)/shard_map/ppermute | solution.py:19
  23.4 15.7 %collective-permute-start.13 = (f32[1,64,512]{2,1,0:T(8,128)S(1)}, f32[1,64,512]{2,1,0:T(8,128)S(1)}, u32[]{:S(2)}, u32[]{:S(2)}) collective-permute-start(f32[1,64,512]{2,1,0:T(8,128)S(1)} %get-tuple-element.43), channel_id=1, source_target_pairs={{0,3},{1,2},{2,1},{3,0},{4,7},{5,6},{6,5},{7,4},{8,11},{9,10},{10,... | collective-permute-start | bytes 393224 | tf_op jit(solution)/shard_map/ppermute | solution.py:19
  23.4 21.5 %collective-permute-start.14 = (f32[1,64,512]{2,1,0:T(8,128)S(1)}, f32[1,64,512]{2,1,0:T(8,128)S(1)}, u32[]{:S(2)}, u32[]{:S(2)}) collective-permute-start(f32[1,64,512]{2,1,0:T(8,128)S(1)} %get-tuple-element.44), channel_id=1, source_target_pairs={{0,1},{1,0},{2,3},{3,2},{4,5},{5,4},{6,7},{7,6},{8,9},{9,8},{10,11... | collective-permute-start | bytes 393224 | tf_op jit(solution)/shard_map/ppermute | solution.py:19
  27.5 17.4 %collective-permute-start.7 = (f32[1,64,512]{2,1,0:T(8,128)S(1)}, f32[1,64,512]{2,1,0:T(8,128)S(1)}, u32[]{:S(2)}, u32[]{:S(2)}) collective-permute-start(f32[1,64,512]{2,1,0:T(8,128)S(1)} %more_first.1), channel_id=1, source_target_pairs={{0,4},{1,5},{2,6},{3,7},{4,0},{5,1},{6,2},{7,3},{8,12},{9,13},{10,... | collective-permute-start | bytes 393224 | tf_op jit(solution)/shard_map/ppermute | solution.py:19
  34.9 12.0 %collective-permute-start.8 = (f32[1,64,512]{2,1,0:T(8,128)S(1)}, f32[1,64,512]{2,1,0:T(8,128)S(1)}, u32[]{:S(2)}, u32[]{:S(2)}) collective-permute-start(f32[1,64,512]{2,1,0:T(8,128)S(1)} %get-tuple-element.37), channel_id=1, source_target_pairs={{0,5},{1,4},{2,7},{3,6},{4,1},{5,0},{6,3},{7,2},{8,13},{9,12},{10,... | collective-permute-start | bytes 393224 | tf_op jit(solution)/shard_map/ppermute | solution.py:19
  35.0 12.8 %copy-start = (f32[1,1,8,64,1024]{4,3,2,1,0:T(8,128)S(1)}, f32[1,1,8,64,1024]{4,3,2,1,0:T(8,128)}, u32[]{:S(2)}) copy-start(f32[1,1,8,64,1024]{4,3,2,1,0:T(8,128)} %param.9) | copy-start | bytes 6291460
  36.9 16.6 %collective-permute-start.4 = (f32[1,64,512]{2,1,0:T(8,128)S(1)}, f32[1,64,512]{2,1,0:T(8,128)S(1)}, u32[]{:S(2)}, u32[]{:S(2)}) collective-permute-start(f32[1,64,512]{2,1,0:T(8,128)S(1)} %get-tuple-element.33), channel_id=1, source_target_pairs={{0,3},{1,2},{2,1},{3,0},{4,7},{5,6},{6,5},{7,4},{8,11},{9,10},{10,... | collective-permute-start | bytes 393224 | tf_op jit(solution)/shard_map/ppermute | solution.py:19
  39.1 13.0 %collective-permute-start.9 = (f32[1,64,512]{2,1,0:T(8,128)S(1)}, f32[1,64,512]{2,1,0:T(8,128)S(1)}, u32[]{:S(2)}, u32[]{:S(2)}) collective-permute-start(f32[1,64,512]{2,1,0:T(8,128)S(1)} %get-tuple-element.38), channel_id=1, source_target_pairs={{0,6},{1,7},{2,4},{3,5},{4,2},{5,3},{6,0},{7,1},{8,14},{9,15},{10,... | collective-permute-start | bytes 393224 | tf_op jit(solution)/shard_map/ppermute | solution.py:19
  44.9 7.7 %collective-permute-start.10 = (f32[1,64,512]{2,1,0:T(8,128)S(1)}, f32[1,64,512]{2,1,0:T(8,128)S(1)}, u32[]{:S(2)}, u32[]{:S(2)}) collective-permute-start(f32[1,64,512]{2,1,0:T(8,128)S(1)} %get-tuple-element.39), channel_id=1, source_target_pairs={{0,2},{1,3},{2,0},{3,1},{4,6},{5,7},{6,4},{7,5},{8,10},{9,11},{10,... | collective-permute-start | bytes 393224 | tf_op jit(solution)/shard_map/ppermute | solution.py:19
  44.9 9.3 %collective-permute-start.5 = (f32[1,64,512]{2,1,0:T(8,128)S(1)}, f32[1,64,512]{2,1,0:T(8,128)S(1)}, u32[]{:S(2)}, u32[]{:S(2)}) collective-permute-start(f32[1,64,512]{2,1,0:T(8,128)S(1)} %get-tuple-element.34), channel_id=1, source_target_pairs={{0,7},{1,6},{2,5},{3,4},{4,3},{5,2},{6,1},{7,0},{8,15},{9,14},{10,... | collective-permute-start | bytes 393224 | tf_op jit(solution)/shard_map/ppermute | solution.py:19
  46.9 9.1 %collective-permute-start.6 = (f32[1,64,512]{2,1,0:T(8,128)S(1)}, f32[1,64,512]{2,1,0:T(8,128)S(1)}, u32[]{:S(2)}, u32[]{:S(2)}) collective-permute-start(f32[1,64,512]{2,1,0:T(8,128)S(1)} %get-tuple-element.35), channel_id=1, source_target_pairs={{0,1},{1,0},{2,3},{3,2},{4,5},{5,4},{6,7},{7,6},{8,9},{9,8},{10,11... | collective-permute-start | bytes 393224 | tf_op jit(solution)/shard_map/ppermute | solution.py:19

commit v3 on v2

--- a/solution.py
+++ b/solution.py
@@ -255,16 +255,21 @@
         for key in keys:
             got[key] = exchange(ready[key], key[0], groups) if key[0] else ready[key]
 
-    a, a2, n, n2 = ([(j, step) for j in some] for some in (far, near[:-1]) for step in range(2))
+    a, a2, n, n2 = ([(j, step) for j in some] for some in (far, (*range(half - 1, 1, -1), 1)) for step in range(2))
     own, own2 = (0, 0), (0, 1)
     send(*ready)
     moved = after(moved, *[got[key] for key in a[:2] + n[:1]])
     ready.update(zip(a2[:1], more("more_first", far_rows, moved, 0, (1,), tile)))
     ready.update(zip(a2[1:], more("more_far", far_rows, moved, 1, ones[1:], tile)))
-    ready.update(zip([*n2, own2], more("more_near", near_rows, moved, 0, ones, tile)))
+    ready.update(zip([(j, 1) for j in near], more("more_near", near_rows, moved, 0, ones, tile)))
     send(*a2, *n2, own2)
     out = None
-    for keys in ([own, *a[:2], *n[:1], *a[2:], *n[1:]], [own2, *a2[:-1], *n2[:1]], [*n2[1:2], a2[-1], *n2[2:]]):
+    plan = (
+        [own, *a[:2], *n[:1], *a[2:], *n[1:]],
+        [own2, *a2[:-1], *n2[-1:]],
+        [*n2[:1], a2[-1], *n2[1:-1]],
+    )
+    for keys in plan:
         out = combine([got[key] for key in keys], [(j, step * cols) for j, step in keys], update, out)
     return out[None, None]
 

time: 57.4 us -> 56.3 us (0.981)
  waiting for transfers between devices: 10.4 us -> 4.67 us
  starting transfers between devices: 30.7 us -> 35.4 us
    ppermute x14, waiting for transfers between devices: 8.98 us -> 3.74 us  [exchange(): return lax.ppermute(piece, 'grid', [(i, i ^ j) for i in range(groups)])]
    ppermute x14, starting transfers between devices: 30.2 us -> 35 us  [exchange(): return lax.ppermute(piece, 'grid', [(i, i ^ j) for i in range(groups)])]
  transfers between devices with their start and end apart: 15 -> 15, of which waited for: 7 -> 4; matrix products, arithmetic and copies ran while one was open for 0% -> 0% of each run, Pallas kernels for 26% -> 27%
where the time goes in v3:
time: 56.3 us; the launch traced here: 55.8 us
  starting transfers between devices  35.4 us (63%)
  Pallas kernels  15.6 us (28%)
  waiting for transfers between devices  4.67 us (8%)
    ppermute x14, starting transfers between devices, exchange(): return lax.ppermute(piece, 'grid', [(i, i ^ j) for i in range(groups)])  35 us
    pallas_call x1, Pallas kernels, second(): pl.pallas_call(functools.partial(second_kernel, skip, js, groups, len(far...  5.21 us
    pallas_call x3, Pallas kernels, more(): pl.pallas_call(functools.partial(more_kernel, skip), out_shape=[jax.Shape...  4.41 us
    ppermute x14, waiting for transfers between devices, exchange(): return lax.ppermute(piece, 'grid', [(i, i ^ j) for i in range(groups)])  3.74 us
    pallas_call x1, Pallas kernels, first(): pl.pallas_call(functools.partial(first_kernel, js, groups), out_shape=[sh...  3.27 us
    pallas_call x3, Pallas kernels, combine(): pl.pallas_call(functools.partial(combine_kernel, tuple(places), out is no...  2.72 us
  transfers between devices with their start and end apart: 15, of which 4 were waited for; matrix products, arithmetic and copies ran while one was open for 0% of the time, Pallas kernels for 27%

profile of v3, /device:TPU:0, one launch (start us, length us, event | category | flops | bytes accessed | tf_op | source)
XLA Modules:
  0.0 55.8 jit_solution(12284830173293470197)
XLA Ops:
  0.0 0.5 collective-permute-start
  0.5 3.3 %first.1 = (f32[1,64,512]{2,1,0:T(8,128)S(1)}, f32[2,256,1024]{2,1,0:T(8,128)S(1)}, bf16[512,1024]{1,0:T(8,128)(2,1)S(1)}, bf16[512,1024]{1,0:T(8,128)(2,1)S(1)}) custom-call(s32[1,1,8]{2,1,0:T(1,128)} %owner_hbm.3, f32[512,1024]{1,0:T(8,128)} %x_hbm.3, f32[512,1024]{1,0:T(8,128)} %z_hbm.3, f32[512,1024]{1,0:T(8,128)} %panel_hbm.1), custom_call_target="tpu_custom_call" | custom-call | flops 402653184 | bytes 4194304 | tf_op jit(solution)/shard_map/first/pallas_call | solution.py:92
  3.7 3.7 %collective-permute-start.1 = (f32[1,64,512]{2,1,0:T(8,128)S(1)}, f32[1,64,512]{2,1,0:T(8,128)S(1)}, u32[]{:S(2)}, u32[]{:S(2)}) collective-permute-start(f32[1,64,512]{2,1,0:T(8,128)S(1)} %get-tuple-element.29), channel_id=1, source_target_pairs={{0,4},{1,5},{2,6},{3,7},{4,0},{5,1},{6,2},{7,3},{8,12},{9,13},{10,... | collective-permute-start | bytes 393224 | tf_op jit(solution)/shard_map/ppermute | solution.py:19
  7.4 5.2 %second.1 = (f32[1,64,512]{2,1,0:T(8,128)S(1)}, f32[1,64,512]{2,1,0:T(8,128)S(1)}, f32[1,64,512]{2,1,0:T(8,128)S(1)}, f32[1,64,512]{2,1,0:T(8,128)S(1)}, f32[1,6...) custom-call(s32[1,1,8]{2,1,0:T(1,128)} %owner_hbm.3, ...), custom_call_target="tpu_custom_call" | custom-call | flops 2818572288 | bytes 5767168 | tf_op jit(solution)/shard_map/second/pallas_call | solution.py:147
  12.6 1.3 %collective-permute-start.2 = (f32[1,64,512]{2,1,0:T(8,128)S(1)}, f32[1,64,512]{2,1,0:T(8,128)S(1)}, u32[]{:S(2)}, u32[]{:S(2)}) collective-permute-start(f32[1,64,512]{2,1,0:T(8,128)S(1)} %get-tuple-element.30), channel_id=1, source_target_pairs={{0,5},{1,4},{2,7},{3,6},{4,1},{5,0},{6,3},{7,2},{8,13},{9,12},{10,... | collective-permute-start | bytes 393224 | tf_op jit(solution)/shard_map/ppermute | solution.py:19
  13.9 1.6 %collective-permute-start.3 = (f32[1,64,512]{2,1,0:T(8,128)S(1)}, f32[1,64,512]{2,1,0:T(8,128)S(1)}, u32[]{:S(2)}, u32[]{:S(2)}) collective-permute-start(f32[1,64,512]{2,1,0:T(8,128)S(1)} %get-tuple-element.31), channel_id=1, source_target_pairs={{0,3},{1,2},{2,1},{3,0},{4,7},{5,6},{6,5},{7,4},{8,11},{9,10},{10,... | collective-permute-start | bytes 393224 | tf_op jit(solution)/shard_map/ppermute | solution.py:19
  15.5 2.5 %collective-permute-start.11 = (f32[1,64,512]{2,1,0:T(8,128)S(1)}, f32[1,64,512]{2,1,0:T(8,128)S(1)}, u32[]{:S(2)}, u32[]{:S(2)}) collective-permute-start(f32[1,64,512]{2,1,0:T(8,128)S(1)} %get-tuple-element.41), channel_id=1, source_target_pairs={{0,6},{1,7},{2,4},{3,5},{4,2},{5,3},{6,0},{7,1},{8,14},{9,15},{10,... | collective-permute-start | bytes 393224 | tf_op jit(solution)/shard_map/ppermute | solution.py:19
  18.0 0.0 collective-permute-done.1.refs_1_
  18.0 4.1 %collective-permute-start.12 = (f32[1,64,512]{2,1,0:T(8,128)S(1)}, f32[1,64,512]{2,1,0:T(8,128)S(1)}, u32[]{:S(2)}, u32[]{:S(2)}) collective-permute-start(f32[1,64,512]{2,1,0:T(8,128)S(1)} %get-tuple-element.42), channel_id=1, source_target_pairs={{0,7},{1,6},{2,5},{3,4},{4,3},{5,2},{6,1},{7,0},{8,15},{9,14},{10,... | collective-permute-start | bytes 393224 | tf_op jit(solution)/shard_map/ppermute | solution.py:19
  22.0 1.3 %collective-permute-done.2.refs_2_ = f32[1,64,512]{2,1,0:T(8,128)S(1)} collective-permute-done((f32[1,64,512]{2,1,0:T(8,128)S(1)}, f32[1,64,512]{2,1,0:T(8,128)S(1)}, u32[]{:S(2)}, u32[]{:S(2)}) %collective-permute-start.2) | collective-permute-done | bytes 131104 | tf_op jit(solution)/shard_map/ppermute | solution.py:19
  23.3 0.8 %collective-permute-start.13 = (f32[1,64,512]{2,1,0:T(8,128)S(1)}, f32[1,64,512]{2,1,0:T(8,128)S(1)}, u32[]{:S(2)}, u32[]{:S(2)}) collective-permute-start(f32[1,64,512]{2,1,0:T(8,128)S(1)} %get-tuple-element.43), channel_id=1, source_target_pairs={{0,2},{1,3},{2,0},{3,1},{4,6},{5,7},{6,4},{7,5},{8,10},{9,11},{10,... | collective-permute-start | bytes 393224 | tf_op jit(solution)/shard_map/ppermute | solution.py:19
  24.1 0.0 collective-permute-done.3.refs_3_
  24.1 1.3 %collective-permute-start.14 = (f32[1,64,512]{2,1,0:T(8,128)S(1)}, f32[1,64,512]{2,1,0:T(8,128)S(1)}, u32[]{:S(2)}, u32[]{:S(2)}) collective-permute-start(f32[1,64,512]{2,1,0:T(8,128)S(1)} %get-tuple-element.44), channel_id=1, source_target_pairs={{0,1},{1,0},{2,3},{3,2},{4,5},{5,4},{6,7},{7,6},{8,9},{9,8},{10,11... | collective-permute-start | bytes 393224 | tf_op jit(solution)/shard_map/ppermute | solution.py:19
  25.4 0.9 %collective-permute-done.panel = f32[512,1024]{1,0:T(8,128)S(1)} collective-permute-done((f32[512,1024]{1,0:T(8,128)}, f32[512,1024]{1,0:T(8,128)S(1)}, u32[]{:S(2)}, u32[]{:S(2)}) %collective-permute-start) | collective-permute-done | bytes 2097184 | tf_op jit(solution)/shard_map/ppermute | solution.py:230
  26.3 1.2 %more_first.1 = f32[1,64,512]{2,1,0:T(8,128)S(1)} custom-call(f32[2,256,1024]{2,1,0:T(8,128)S(1)} %get-tuple-element.25.rows, f32[512,1024]{1,0:T(8,128)S(1)} %collective-permute-done.panel), custom_call_target="tpu_custom_call" | custom-call | flops 402653184 | bytes 2621440 | tf_op jit(solution)/shard_map/more_first/pallas_call | solution.py:176
  27.5 5.7 %collective-permute-start.7 = (f32[1,64,512]{2,1,0:T(8,128)S(1)}, f32[1,64,512]{2,1,0:T(8,128)S(1)}, u32[]{:S(2)}, u32[]{:S(2)}) collective-permute-start(f32[1,64,512]{2,1,0:T(8,128)S(1)} %more_first.1), channel_id=1, source_target_pairs={{0,4},{1,5},{2,6},{3,7},{4,0},{5,1},{6,2},{7,3},{8,12},{9,13},{10,... | collective-permute-start | bytes 393224 | tf_op jit(solution)/shard_map/ppermute | solution.py:19
  33.2 1.4 %more_far.1 = (f32[1,64,512]{2,1,0:T(8,128)S(1)}, f32[1,64,512]{2,1,0:T(8,128)S(1)}, f32[1,64,512]{2,1,0:T(8,128)S(1)}) custom-call(f32[2,256,1024]{2,1,0:T(8,128)S(1)} %get-tuple-element.25.rows, f32[512,1024]{1,0:T(8,128)S(1)} %collective-permute-done.panel), custom_call_target="tpu_custom_call" | custom-call | flops 1207959552 | bytes 3670016 | tf_op jit(solution)/shard_map/more_far/pallas_call | solution.py:176
  34.6 0.0 collective-permute-done.11.refs_4_
  34.6 0.1 collective-permute-start.8
  34.7 0.0 copy-start
  34.7 1.8 %more_near.1 = (f32[1,64,512]{2,1,0:T(8,128)S(1)}, f32[1,64,512]{2,1,0:T(8,128)S(1)}, f32[1,64,512]{2,1,0:T(8,128)S(1)}, f32[1,64,512]{2,1,0:T(8,128)S(1)}) custom-call(f32[2,256,1024]{2,1,0:T(8,128)S(1)} %get-tuple-element.28.rows, f32[512,1024]{1,0:T(8,128)S(1)} %collective-permute-done.panel), custom_call_target="tpu_custom_call" | custom-call | flops 1610612736 | bytes 4194304 | tf_op jit(solution)/shard_map/more_near/pallas_call | solution.py:176
  36.6 0.0 collective-permute-done.12.refs_5_
  36.6 3.4 %collective-permute-start.4 = (f32[1,64,512]{2,1,0:T(8,128)S(1)}, f32[1,64,512]{2,1,0:T(8,128)S(1)}, u32[]{:S(2)}, u32[]{:S(2)}) collective-permute-start(f32[1,64,512]{2,1,0:T(8,128)S(1)} %get-tuple-element.33), channel_id=1, source_target_pairs={{0,3},{1,2},{2,1},{3,0},{4,7},{5,6},{6,5},{7,4},{8,11},{9,10},{10,... | collective-permute-start | bytes 393224 | tf_op jit(solution)/shard_map/ppermute | solution.py:19
  40.0 0.0 collective-permute-done.13.refs_6_
  40.0 2.4 %collective-permute-start.9 = (f32[1,64,512]{2,1,0:T(8,128)S(1)}, f32[1,64,512]{2,1,0:T(8,128)S(1)}, u32[]{:S(2)}, u32[]{:S(2)}) collective-permute-start(f32[1,64,512]{2,1,0:T(8,128)S(1)} %get-tuple-element.38), channel_id=1, source_target_pairs={{0,6},{1,7},{2,4},{3,5},{4,2},{5,3},{6,0},{7,1},{8,14},{9,15},{10,... | collective-permute-start | bytes 393224 | tf_op jit(solution)/shard_map/ppermute | solution.py:19
  42.4 0.0 collective-permute-done.14.refs_7_
  42.4 0.0 collective-permute-start.10
  42.4 0.0 collective-permute-done.7.refs_1_
  42.5 3.3 %collective-permute-start.5 = (f32[1,64,512]{2,1,0:T(8,128)S(1)}, f32[1,64,512]{2,1,0:T(8,128)S(1)}, u32[]{:S(2)}, u32[]{:S(2)}) collective-permute-start(f32[1,64,512]{2,1,0:T(8,128)S(1)} %get-tuple-element.34), channel_id=1, source_target_pairs={{0,7},{1,6},{2,5},{3,4},{4,3},{5,2},{6,1},{7,0},{8,15},{9,14},{10,... | collective-permute-start | bytes 393224 | tf_op jit(solution)/shard_map/ppermute | solution.py:19
  45.7 0.9 %collective-permute-done.8.refs_2_ = f32[1,64,512]{2,1,0:T(8,128)S(1)} collective-permute-done((f32[1,64,512]{2,1,0:T(8,128)S(1)}, f32[1,64,512]{2,1,0:T(8,128)S(1)}, u32[]{:S(2)}, u32[]{:S(2)}) %collective-permute-start.8) | collective-permute-done | bytes 131104 | tf_op jit(solution)/shard_map/ppermute | solution.py:19
  46.6 4.9 %collective-permute-start.6 = (f32[1,64,512]{2,1,0:T(8,128)S(1)}, f32[1,64,512]{2,1,0:T(8,128)S(1)}, u32[]{:S(2)}, u32[]{:S(2)}) collective-permute-start(f32[1,64,512]{2,1,0:T(8,128)S(1)} %get-tuple-element.35), channel_id=1, source_target_pairs={{0,2},{1,3},{2,0},{3,1},{4,6},{5,7},{6,4},{7,5},{8,10},{9,11},{10,... | collective-permute-start | bytes 393224 | tf_op jit(solution)/shard_map/ppermute | solution.py:19
  51.6 0.0 copy-done
  51.6 1.0 %combine.3.refs_6_ = f32[8,64,1024]{2,1,0:T(8,128)} custom-call(f32[1,64,512]{2,1,0:T(8,128)S(1)} %get-tuple-element.40.refs_0_, f32[1,64,512]{2,1,0:T(8,128)S(1)} %collective-permute-done.1.refs_1_, f32[1,64,512]{2,1,0:T(8,128)S(1)} %collective-permute-done.2.refs_2_, f32[1,64,512]{2,1,0:T(8,128)S(1)} %collective-permute-done.3.refs_3_, ...), custom_call_target="tpu_custom_call" | custom-call | flops 262144 | bytes 3145728 | tf_op jit(solution)/shard_map/combine/pallas_call | solution.py:211
  52.6 0.0 collective-permute-done.9.refs_3_
  52.7 0.0 collective-permute-done.10.refs_4_
  52.7 0.9 %combine.4.refs_4_ = f32[8,64,1024]{2,1,0:T(8,128)} custom-call(f32[1,64,512]{2,1,0:T(8,128)S(1)} %get-tuple-element.36.refs_0_, f32[1,64,512]{2,1,0:T(8,128)S(1)} %collective-permute-done.7.refs_1_, f32[1,64,512]{2,1,0:T(8,128)S(1)} %collective-permute-done.8.refs_2_, ...), custom_call_target="tpu_custom_call", output_to_operand_aliasing={{}: (6, {})} | custom-call | flops 163840 | bytes 1966080 | tf_op jit(solution)/shard_map/combine/pallas_call | solution.py:211
  53.6 0.0 collective-permute-done.4.refs_0_
  53.6 0.0 collective-permute-done.5.refs_1_
  53.6 1.5 %collective-permute-done.6.refs_2_ = f32[1,64,512]{2,1,0:T(8,128)S(1)} collective-permute-done((f32[1,64,512]{2,1,0:T(8,128)S(1)}, f32[1,64,512]{2,1,0:T(8,128)S(1)}, u32[]{:S(2)}, u32[]{:S(2)}) %collective-permute-start.6) | collective-permute-done | bytes 131104 | tf_op jit(solution)/shard_map/ppermute | solution.py:19
  55.1 0.8 %combine.5 = f32[8,64,1024]{2,1,0:T(8,128)} custom-call(f32[1,64,512]{2,1,0:T(8,128)S(1)} %collective-permute-done.4.refs_0_, f32[1,64,512]{2,1,0:T(8,128)S(1)} %collective-permute-done.5.refs_1_, f32[1,64,512]{2,1,0:T(8,128)S(1)} %collective-permute-done.6.refs_2_, f32[8,64,1024]{2,1,0:T(8,128)S(1)} %bitcast.4, ...), custom_call_target="tpu_custom_call", output_to_operand_aliasing={{}: (4, {})} | custom-call | flops 98304 | bytes 1179648 | tf_op jit(solution)/shard_map/combine/pallas_call | solution.py:211
Async XLA Ops:
  0.0 26.3 %collective-permute-start = (f32[512,1024]{1,0:T(8,128)}, f32[512,1024]{1,0:T(8,128)S(1)}, u32[]{:S(2)}, u32[]{:S(2)}) collective-permute-start(f32[512,1024]{1,0:T(8,128)} %panel_hbm.1), channel_id=1, source_target_pairs={{0,8},{8,16},{16,24},{24,0},{1,9},{9,17},{17,25},{25,1},{2,10},{10... | collective-permute-start | bytes 6291464 | tf_op jit(solution)/shard_map/ppermute | solution.py:230
  3.7 14.2 %collective-permute-start.1 = (f32[1,64,512]{2,1,0:T(8,128)S(1)}, f32[1,64,512]{2,1,0:T(8,128)S(1)}, u32[]{:S(2)}, u32[]{:S(2)}) collective-permute-start(f32[1,64,512]{2,1,0:T(8,128)S(1)} %get-tuple-element.29), channel_id=1, source_target_pairs={{0,4},{1,5},{2,6},{3,7},{4,0},{5,1},{6,2},{7,3},{8,12},{9,13},{10,... | collective-permute-start | bytes 393224 | tf_op jit(solution)/shard_map/ppermute | solution.py:19
  12.6 10.7 %collective-permute-start.2 = (f32[1,64,512]{2,1,0:T(8,128)S(1)}, f32[1,64,512]{2,1,0:T(8,128)S(1)}, u32[]{:S(2)}, u32[]{:S(2)}) collective-permute-start(f32[1,64,512]{2,1,0:T(8,128)S(1)} %get-tuple-element.30), channel_id=1, source_target_pairs={{0,5},{1,4},{2,7},{3,6},{4,1},{5,0},{6,3},{7,2},{8,13},{9,12},{10,... | collective-permute-start | bytes 393224 | tf_op jit(solution)/shard_map/ppermute | solution.py:19
  13.9 10.2 %collective-permute-start.3 = (f32[1,64,512]{2,1,0:T(8,128)S(1)}, f32[1,64,512]{2,1,0:T(8,128)S(1)}, u32[]{:S(2)}, u32[]{:S(2)}) collective-permute-start(f32[1,64,512]{2,1,0:T(8,128)S(1)} %get-tuple-element.31), channel_id=1, source_target_pairs={{0,3},{1,2},{2,1},{3,0},{4,7},{5,6},{6,5},{7,4},{8,11},{9,10},{10,... | collective-permute-start | bytes 393224 | tf_op jit(solution)/shard_map/ppermute | solution.py:19
  15.5 19.1 %collective-permute-start.11 = (f32[1,64,512]{2,1,0:T(8,128)S(1)}, f32[1,64,512]{2,1,0:T(8,128)S(1)}, u32[]{:S(2)}, u32[]{:S(2)}) collective-permute-start(f32[1,64,512]{2,1,0:T(8,128)S(1)} %get-tuple-element.41), channel_id=1, source_target_pairs={{0,6},{1,7},{2,4},{3,5},{4,2},{5,3},{6,0},{7,1},{8,14},{9,15},{10,... | collective-permute-start | bytes 393224 | tf_op jit(solution)/shard_map/ppermute | solution.py:19
  18.0 18.6 %collective-permute-start.12 = (f32[1,64,512]{2,1,0:T(8,128)S(1)}, f32[1,64,512]{2,1,0:T(8,128)S(1)}, u32[]{:S(2)}, u32[]{:S(2)}) collective-permute-start(f32[1,64,512]{2,1,0:T(8,128)S(1)} %get-tuple-element.42), channel_id=1, source_target_pairs={{0,7},{1,6},{2,5},{3,4},{4,3},{5,2},{6,1},{7,0},{8,15},{9,14},{10,... | collective-permute-start | bytes 393224 | tf_op jit(solution)/shard_map/ppermute | solution.py:19
  23.3 16.7 %collective-permute-start.13 = (f32[1,64,512]{2,1,0:T(8,128)S(1)}, f32[1,64,512]{2,1,0:T(8,128)S(1)}, u32[]{:S(2)}, u32[]{:S(2)}) collective-permute-start(f32[1,64,512]{2,1,0:T(8,128)S(1)} %get-tuple-element.43), channel_id=1, source_target_pairs={{0,2},{1,3},{2,0},{3,1},{4,6},{5,7},{6,4},{7,5},{8,10},{9,11},{10,... | collective-permute-start | bytes 393224 | tf_op jit(solution)/shard_map/ppermute | solution.py:19
  24.1 18.3 %collective-permute-start.14 = (f32[1,64,512]{2,1,0:T(8,128)S(1)}, f32[1,64,512]{2,1,0:T(8,128)S(1)}, u32[]{:S(2)}, u32[]{:S(2)}) collective-permute-start(f32[1,64,512]{2,1,0:T(8,128)S(1)} %get-tuple-element.44), channel_id=1, source_target_pairs={{0,1},{1,0},{2,3},{3,2},{4,5},{5,4},{6,7},{7,6},{8,9},{9,8},{10,11... | collective-permute-start | bytes 393224 | tf_op jit(solution)/shard_map/ppermute | solution.py:19
  27.5 15.0 %collective-permute-start.7 = (f32[1,64,512]{2,1,0:T(8,128)S(1)}, f32[1,64,512]{2,1,0:T(8,128)S(1)}, u32[]{:S(2)}, u32[]{:S(2)}) collective-permute-start(f32[1,64,512]{2,1,0:T(8,128)S(1)} %more_first.1), channel_id=1, source_target_pairs={{0,4},{1,5},{2,6},{3,7},{4,0},{5,1},{6,2},{7,3},{8,12},{9,13},{10,... | collective-permute-start | bytes 393224 | tf_op jit(solution)/shard_map/ppermute | solution.py:19
  34.6 12.0 %collective-permute-start.8 = (f32[1,64,512]{2,1,0:T(8,128)S(1)}, f32[1,64,512]{2,1,0:T(8,128)S(1)}, u32[]{:S(2)}, u32[]{:S(2)}) collective-permute-start(f32[1,64,512]{2,1,0:T(8,128)S(1)} %get-tuple-element.37), channel_id=1, source_target_pairs={{0,5},{1,4},{2,7},{3,6},{4,1},{5,0},{6,3},{7,2},{8,13},{9,12},{10,... | collective-permute-start | bytes 393224 | tf_op jit(solution)/shard_map/ppermute | solution.py:19
  34.7 16.9 %copy-start = (f32[1,1,8,64,1024]{4,3,2,1,0:T(8,128)S(1)}, f32[1,1,8,64,1024]{4,3,2,1,0:T(8,128)}, u32[]{:S(2)}) copy-start(f32[1,1,8,64,1024]{4,3,2,1,0:T(8,128)} %param.9) | copy-start | bytes 6291460
  36.6 17.0 %collective-permute-start.4 = (f32[1,64,512]{2,1,0:T(8,128)S(1)}, f32[1,64,512]{2,1,0:T(8,128)S(1)}, u32[]{:S(2)}, u32[]{:S(2)}) collective-permute-start(f32[1,64,512]{2,1,0:T(8,128)S(1)} %get-tuple-element.33), channel_id=1, source_target_pairs={{0,3},{1,2},{2,1},{3,0},{4,7},{5,6},{6,5},{7,4},{8,11},{9,10},{10,... | collective-permute-start | bytes 393224 | tf_op jit(solution)/shard_map/ppermute | solution.py:19
  40.0 12.6 %collective-permute-start.9 = (f32[1,64,512]{2,1,0:T(8,128)S(1)}, f32[1,64,512]{2,1,0:T(8,128)S(1)}, u32[]{:S(2)}, u32[]{:S(2)}) collective-permute-start(f32[1,64,512]{2,1,0:T(8,128)S(1)} %get-tuple-element.38), channel_id=1, source_target_pairs={{0,6},{1,7},{2,4},{3,5},{4,2},{5,3},{6,0},{7,1},{8,14},{9,15},{10,... | collective-permute-start | bytes 393224 | tf_op jit(solution)/shard_map/ppermute | solution.py:19
  42.4 10.2 %collective-permute-start.10 = (f32[1,64,512]{2,1,0:T(8,128)S(1)}, f32[1,64,512]{2,1,0:T(8,128)S(1)}, u32[]{:S(2)}, u32[]{:S(2)}) collective-permute-start(f32[1,64,512]{2,1,0:T(8,128)S(1)} %get-tuple-element.39), channel_id=1, source_target_pairs={{0,1},{1,0},{2,3},{3,2},{4,5},{5,4},{6,7},{7,6},{8,9},{9,8},{10,11... | collective-permute-start | bytes 393224 | tf_op jit(solution)/shard_map/ppermute | solution.py:19
  42.5 11.1 %collective-permute-start.5 = (f32[1,64,512]{2,1,0:T(8,128)S(1)}, f32[1,64,512]{2,1,0:T(8,128)S(1)}, u32[]{:S(2)}, u32[]{:S(2)}) collective-permute-start(f32[1,64,512]{2,1,0:T(8,128)S(1)} %get-tuple-element.34), channel_id=1, source_target_pairs={{0,7},{1,6},{2,5},{3,4},{4,3},{5,2},{6,1},{7,0},{8,15},{9,14},{10,... | collective-permute-start | bytes 393224 | tf_op jit(solution)/shard_map/ppermute | solution.py:19
  46.6 8.4 %collective-permute-start.6 = (f32[1,64,512]{2,1,0:T(8,128)S(1)}, f32[1,64,512]{2,1,0:T(8,128)S(1)}, u32[]{:S(2)}, u32[]{:S(2)}) collective-permute-start(f32[1,64,512]{2,1,0:T(8,128)S(1)} %get-tuple-element.35), channel_id=1, source_target_pairs={{0,2},{1,3},{2,0},{3,1},{4,6},{5,7},{6,4},{7,5},{8,10},{9,11},{10,... | collective-permute-start | bytes 393224 | tf_op jit(solution)/shard_map/ppermute | solution.py:19
